TPU v7x, 32 devices: a whole 2x2x4 slice. The times are simulated.
32 devices in a mesh: dp: 16 (over z, y, x), mp: 2 (over core).
Axes of the slice: x: 2, y: 2, z: 4, core: 2. Of those that a mesh axis runs over, the one named last changes fastest.
Arguments:
- tokens: bfloat16 [8192, 768], P('dp'), may hold values from -6 to 6
- lengths: int32 [16], P('dp'), may hold values from 40 to 512, as said below
- cotangent: bfloat16 [8192, 768], P('dp'), may hold values from -6 to 6
- query_weight: bfloat16 [768, 768], P(None, 'mp'), may hold values from -0.21875 to 0.21875
- query_bias: bfloat16 [768], P('mp'), may hold values from -3 to 3
- key_weight: bfloat16 [768, 768], P(None, 'mp'), may hold values from -0.21875 to 0.21875
- value_weight: bfloat16 [768, 768], P(None, 'mp'), may hold values from -0.21875 to 0.21875
- value_bias: bfloat16 [768], P('mp'), may hold values from -1 to 1
- out_weight: bfloat16 [768, 768], P('mp'), may hold values from -1.75 to 1.75
- out_bias: bfloat16 [768], replicated, may hold values from -3 to 3
- mid_gain: bfloat16 [768], replicated, may hold values from 0.5 to 1.5
- mid_shift: bfloat16 [768], replicated, may hold values from -3 to 3
- up_weight: bfloat16 [768, 3072], P(None, 'mp'), may hold values from -0.21875 to 0.21875
- up_bias: bfloat16 [3072], P('mp'), may hold values from -3 to 3
- down_weight: bfloat16 [3072, 768], P('mp'), may hold values from -0.15625 to 0.15625
- down_bias: bfloat16 [768], replicated, may hold values from -3 to 3
- final_gain: bfloat16 [768], replicated, may hold values from 0.5 to 1.5
- final_shift: bfloat16 [768], replicated, may hold values from -3 to 3
Outputs:
- layer_out: bfloat16 [8192, 768], P('dp')
- input_grad: bfloat16 [8192, 768], P('dp')
- query_weight_grad: float32 [768, 768], P(None, 'mp')
- query_bias_grad: float32 [768], P('mp')
- key_weight_grad: float32 [768, 768], P(None, 'mp')
- value_weight_grad: float32 [768, 768], P(None, 'mp')
- value_bias_grad: float32 [768], P('mp')
- out_weight_grad: float32 [768, 768], P('mp')
- out_bias_grad: float32 [768], replicated
- mid_gain_grad: float32 [768], replicated
- mid_shift_grad: float32 [768], replicated
- up_weight_grad: float32 [768, 3072], P(None, 'mp')
- up_bias_grad: float32 [3072], P('mp')
- down_weight_grad: float32 [3072, 768], P('mp')
- down_bias_grad: float32 [768], replicated
- final_gain_grad: float32 [768], replicated
- final_shift_grad: float32 [768], replicated
Inputs may be any that keep to these rules, and one draw needn't show every extreme that they name: `lengths`: real tokens of each page; key slots at or beyond it are padding. Some page has exactly 512 and some exactly 40.
All inputs are finite; a program needn't handle non-finite values.
Results may differ from a plain program's by a relative error of at most 0.015.
The roundings to bfloat16 on the way count: a program that leaves them out, or rounds other values in their place, can miss the bound.
Values sent between devices are 32-bit elements; how exact they have to be, the bound alone decides.
No kernel may reach another device: no remote copies, remote signals or barrier semaphores. Data moves between devices by JAX's collectives and lax.ppermute only.
A program may use at most 128 MiB of HBM per device.

v0:
```python
import jax
import jax.numpy as jnp
from jax import lax
from jax.sharding import PartitionSpec as P

DH = 64


norm_eps = 1e-12
score_scale = 0.125
root_half = 0.7071067811865476
inv_root_two_pi = 0.3989422804014327


def matmul(left, right):
    return jnp.dot(left, right, preferred_element_type=jnp.float32)


def matmul_flip(left, right):
    return lax.dot_general(
        left, right, (((1,), (1,)), ((), ())), preferred_element_type=jnp.float32
    )


def outer_sum(left, right):
    return lax.dot_general(
        left, right, (((0,), (0,)), ((), ())), preferred_element_type=jnp.float32
    )


def norm_forward(value, gain, shift):
    center = value - jnp.mean(value, axis=-1, keepdims=True)
    scale = lax.rsqrt(jnp.mean(center * center, axis=-1, keepdims=True) + norm_eps)
    normal = center * scale
    return (normal * gain.astype(jnp.float32) + shift.astype(jnp.float32), normal, scale)


def norm_backward(upper, normal, scale, gain):
    along = upper * gain.astype(jnp.float32)
    lower = scale * (
        along
        - jnp.mean(along, axis=-1, keepdims=True)
        - normal * jnp.mean(along * normal, axis=-1, keepdims=True)
    )
    return (lower, jnp.sum(upper * normal, axis=0), jnp.sum(upper, axis=0))


def masked_scores(query, keys, limit):
    scores = (
        jnp.einsum("qhd,khd->hqk", query, keys, preferred_element_type=jnp.float32) * score_scale
    )
    visible = lax.iota(jnp.int32, keys.shape[0]) < limit
    return jnp.where(visible[None, None, :], scores, -1e30)


def attend_page(item):
    query, keys, values, limit = item
    scores = masked_scores(query, keys, limit)
    top = jnp.max(scores, axis=-1, keepdims=True)
    raised = jnp.exp(scores - top)
    total = jnp.sum(raised, axis=-1, keepdims=True)
    chances = (raised / total).astype(jnp.bfloat16)
    context = jnp.einsum("hqk,khd->qhd", chances, values, preferred_element_type=jnp.float32)
    return (context.astype(jnp.bfloat16), top + jnp.log(total))


def attend_back(item):
    query, keys, values, limit, log_total, upstream = item
    chances = jnp.exp(masked_scores(query, keys, limit) - log_total)
    rounded = chances.astype(jnp.bfloat16)
    value_grad = jnp.einsum("hqk,qhd->khd", rounded, upstream, preferred_element_type=jnp.float32)
    spread = jnp.einsum("qhd,khd->hqk", upstream, values, preferred_element_type=jnp.float32)
    spread = lax.optimization_barrier(spread.astype(jnp.bfloat16)).astype(jnp.float32)
    score_grad = chances * (spread - jnp.sum(spread * chances, axis=-1, keepdims=True))
    score_grad = score_grad.astype(jnp.bfloat16)
    query_grad = (
        jnp.einsum("hqk,khd->qhd", score_grad, keys, preferred_element_type=jnp.float32)
        * score_scale
    )
    key_grad = (
        jnp.einsum("hqk,qhd->khd", score_grad, query, preferred_element_type=jnp.float32)
        * score_scale
    )
    return (
        query_grad.astype(jnp.bfloat16),
        key_grad.astype(jnp.bfloat16),
        value_grad.astype(jnp.bfloat16),
    )


def gelu_slope(before):
    return 0.5 * (1.0 + lax.erf(before * root_half)) + before * inv_root_two_pi * jnp.exp(
        -0.5 * before * before
    )


def flatten(grads):
    return jnp.concatenate([grad.reshape(-1) for grad in grads])


def unflatten(flat, grads):
    pieces = []
    offset = 0
    for grad in grads:
        count = grad.size
        pieces.append(flat[offset : offset + count].reshape(grad.shape))
        offset = offset + count
    return tuple(pieces)


def body(
    tokens,
    lengths,
    cotangent,
    query_weight,
    query_bias,
    key_weight,
    value_weight,
    value_bias,
    out_weight,
    out_bias,
    mid_gain,
    mid_shift,
    up_weight,
    up_bias,
    down_weight,
    down_bias,
    final_gain,
    final_shift,
):
    rows = tokens.shape[0]
    pages = lengths.shape[0]
    length = rows // pages
    heads = query_weight.shape[1] // DH

    def by_page(matrix):
        return matrix.reshape(pages, length, heads, DH)

    query = (matmul(tokens, query_weight) + query_bias.astype(jnp.float32)).astype(jnp.bfloat16)
    keys = matmul(tokens, key_weight).astype(jnp.bfloat16)
    values = (matmul(tokens, value_weight) + value_bias.astype(jnp.float32)).astype(jnp.bfloat16)
    context, log_total = lax.map(
        attend_page, (by_page(query), by_page(keys), by_page(values), lengths)
    )
    context = context.reshape(rows, heads * DH)
    attended = lax.psum(matmul(context, out_weight), "mp")
    inputs = tokens.astype(jnp.float32)
    middle, mid_normal, mid_scale = norm_forward(
        inputs + attended + out_bias.astype(jnp.float32), mid_gain, mid_shift
    )
    mid_low = middle.astype(jnp.bfloat16)
    before = matmul(mid_low, up_weight) + up_bias.astype(jnp.float32)
    active = jax.nn.gelu(before, approximate=False).astype(jnp.bfloat16)
    down = lax.psum(matmul(active, down_weight), "mp")
    result, final_normal, final_scale = norm_forward(
        middle + down + down_bias.astype(jnp.float32), final_gain, final_shift
    )
    layer_out = result.astype(jnp.bfloat16)
    upper = cotangent.astype(jnp.float32)
    second_grad, final_gain_grad, final_shift_grad = norm_backward(
        upper, final_normal, final_scale, final_gain
    )
    down_bias_grad = jnp.sum(second_grad, axis=0)
    second_low = second_grad.astype(jnp.bfloat16)
    down_weight_grad = outer_sum(active, second_low)
    before_grad = (matmul_flip(second_low, down_weight) * gelu_slope(before)).astype(jnp.bfloat16)
    up_weight_grad = outer_sum(mid_low, before_grad)
    up_bias_grad = jnp.sum(before_grad.astype(jnp.float32), axis=0)
    mid_grad = second_grad + lax.psum(matmul_flip(before_grad, up_weight), "mp")
    first_grad, mid_gain_grad, mid_shift_grad = norm_backward(
        mid_grad, mid_normal, mid_scale, mid_gain
    )
    out_bias_grad = jnp.sum(first_grad, axis=0)
    first_low = first_grad.astype(jnp.bfloat16)
    out_weight_grad = outer_sum(context, first_low)
    context_grad = matmul_flip(first_low, out_weight).astype(jnp.bfloat16)
    ffn_grads = (
        mid_gain_grad,
        mid_shift_grad,
        up_weight_grad,
        up_bias_grad,
        down_weight_grad,
        down_bias_grad,
        final_gain_grad,
        final_shift_grad,
    )
    query_grad, key_grad, value_grad = lax.map(
        attend_back,
        (by_page(query), by_page(keys), by_page(values), lengths, log_total, by_page(context_grad)),
    )
    query_grad = query_grad.reshape(rows, heads * DH)
    key_grad = key_grad.reshape(rows, heads * DH)
    value_grad = value_grad.reshape(rows, heads * DH)
    query_weight_grad = outer_sum(tokens, query_grad)
    query_bias_grad = jnp.sum(query_grad.astype(jnp.float32), axis=0)
    key_weight_grad = outer_sum(tokens, key_grad)
    value_weight_grad = outer_sum(tokens, value_grad)
    value_bias_grad = jnp.sum(value_grad.astype(jnp.float32), axis=0)
    input_part = (
        matmul_flip(query_grad, query_weight)
        + matmul_flip(key_grad, key_weight)
        + matmul_flip(value_grad, value_weight)
    )
    input_grad = (first_grad + lax.psum(input_part, "mp")).astype(jnp.bfloat16)
    attn_grads = (
        query_weight_grad,
        query_bias_grad,
        key_weight_grad,
        value_weight_grad,
        value_bias_grad,
        out_weight_grad,
        out_bias_grad,
    )
    every = attn_grads + ffn_grads
    summed = unflatten(lax.psum(flatten(every), "dp"), every)
    return (
        layer_out,
        input_grad,
        summed[0],
        summed[1],
        summed[2],
        summed[3],
        summed[4],
        summed[5],
        summed[6],
        summed[7],
        summed[8],
        summed[9],
        summed[10],
        summed[11],
        summed[12],
        summed[13],
        summed[14],
    )


def solution(mesh):
    in_specs = (
        P("dp", None),
        P("dp"),
        P("dp", None),
        P(None, "mp"),
        P("mp"),
        P(None, "mp"),
        P(None, "mp"),
        P("mp"),
        P("mp", None),
        P(),
        P(),
        P(),
        P(None, "mp"),
        P("mp"),
        P("mp", None),
        P(),
        P(),
        P(),
    )
    out_specs = (
        P("dp", None),
        P("dp", None),
        P(None, "mp"),
        P("mp"),
        P(None, "mp"),
        P(None, "mp"),
        P("mp"),
        P("mp", None),
        P(),
        P(),
        P(),
        P(None, "mp"),
        P("mp"),
        P("mp", None),
        P(),
        P(),
        P(),
    )
    return jax.shard_map(body, mesh=mesh, in_specs=in_specs, out_specs=out_specs, check_vma=False)
```

profile of v0, /device:TPU:0, one launch (start us, length us, event | category | flops | bytes accessed | tf_op | source)
XLA Modules:
  0.0 675.6 jit_solution(18103086827341132360)
XLA Ops:
  9.5 1.8 convolution_convert_fusion.2
  11.4 1.8 fusion.31
  13.7 1.5 fusion.57
  16.2 1.7 copy-done.2
  19.9 1.7 fusion.58
  23.0 21.9 %all-reduce.6.cloned.1.call-done = f32[512,768]{1,0:T(8,128)} async-done(((f32[512,768]{1,0:T(8,128)}), f32[512,768]{1,0:T(8,128)}) %all-reduce.6.cloned.1.call-update) | async-done | bytes 1572880 | tf_op jit(solution)/shard_map/psum | solution.py:146
  44.9 1.7 fusion.52
  47.0 9.1 %fusion.7 = (bf16[512,1536]{1,0:T(8,128)(2,1)S(1)}, f32[512,1536]{1,0:T(8,128)}) fusion(f32[1536]{0:T(1024)S(1)} %copy-done.47, bf16[768,1536]{1,0:T(8,128)(2,1)S(1)} %copy-done, f32[512,768]{1,0:T(8,128)S(1)} %get-tuple-element.84, f32[768]{0:T(1024)S(1)} %convert_element_type.138, f32[768]{0:T(1024)S(1)} %convert_element_type.137, ...), kind=kOutput, calls=%fused_computation.17 | convolution fusion | flops 1261830144 | bytes 8667136 | tf_op jit(solution)/shard_map/dot_general | solution.py:16
  57.3 2.5 fusion.59
  62.6 18.9 %all-reduce.8.cloned.1.call-done = f32[512,768]{1,0:T(8,128)} async-done(((f32[512,768]{1,0:T(8,128)}), f32[512,768]{1,0:T(8,128)}) %all-reduce.8.cloned.1.call-update) | async-done | bytes 1572880 | tf_op jit(solution)/shard_map/psum | solution.py:154
  81.6 2.5 fusion.51
  84.5 1.3 fusion.29
  85.8 2.1 fusion.48
  88.0 3.3 convert_reduce_fusion
  92.4 2.6 fusion.60
  95.8 5.7 fusion.45
  101.5 6.0 reshape.203
  107.6 5.0 fusion.42
  112.6 6.0 reshape.204
  118.6 3.4 multiply_reduce_fusion
  126.0 1.4 fusion.2
  129.7 1.8 convert_reduce_fusion.2
  132.1 1.5 convolution_bitcast_fusion.2
  134.2 1.5 convolution_bitcast_fusion.1
  135.7 1.5 fusion.39
  137.2 1.5 convolution_bitcast_fusion
  138.7 1.7 add_add_fusion
  142.4 1.4 copy.46
  143.8 1.4 reshape.200
  145.3 1.4 copy.47
  146.7 2.5 reshape.201
  149.3 1.4 constant_dynamic-update-slice_fusion.9
  150.7 10.9 %dynamic-update-slice.2 = f32[3545856]{0:T(1024)} dynamic-update-slice(f32[3545856]{0:T(1024)} %constant_dynamic-update-slice_fusion.9, f32[294912]{0:T(1024)S(1)} %reshape.200, s32[]{} %constant.126) | dynamic-update-slice | bytes 2359300
  161.6 10.9 %dynamic-update-slice.3 = f32[3545856]{0:T(1024)} dynamic-update-slice(f32[3545856]{0:T(1024)} %dynamic-update-slice.2, f32[294912]{0:T(1024)S(1)} %copy-done.14, s32[]{} %constant.127) | dynamic-update-slice | bytes 2359300
  173.8 10.9 %dynamic-update-slice.5 = f32[3545856]{0:T(1024)} dynamic-update-slice(f32[3545856]{0:T(1024)} %constant_dynamic-update-slice_fusion.8, f32[294912]{0:T(1024)S(1)} %reshape.202, s32[]{} %constant.129) | dynamic-update-slice | bytes 2359300
  184.7 1.3 constant_dynamic-update-slice_fusion.7
  188.6 4.0 constant_dynamic-update-slice_fusion.4
  192.6 1.3 constant_dynamic-update-slice_fusion.3
  193.9 41.0 %dynamic-update-slice.11 = f32[3545856]{0:T(1024)} dynamic-update-slice(f32[3545856]{0:T(1024)} %constant_dynamic-update-slice_fusion.3, f32[1179648]{0:T(1024)} %reshape.204, s32[]{} %constant.135) | dynamic-update-slice | bytes 9437188
  238.1 1.4 copy-done.6
  239.4 2.4 add_convert_fusion
  241.9 395.0 %all-reduce.14.cloned.1.call-done = f32[3545856]{0:T(1024)} async-done(((f32[3545856]{0:T(1024)}), f32[3545856]{0:T(1024)}) %all-reduce.14.cloned.1.call-update) | async-done | bytes 14183440 | tf_op jit(solution)/shard_map/psum | solution.py:215
  636.9 3.6 fusion.55
  640.5 2.5 slice.96
  646.8 6.4 fusion.54
  653.2 5.8 reshape.205
  659.0 6.1 slice.111
  666.4 1.4 fusion.53
  (177 shorter events, 36.1 us)
Async XLA Ops:
  7.2 39.8 %copy-start = (bf16[768,1536]{1,0:T(8,128)(2,1)S(1)}, bf16[768,1536]{1,0:T(8,128)(2,1)}, u32[]{:S(2)}) copy-start(bf16[768,1536]{1,0:T(8,128)(2,1)} %param.30) | copy-start | bytes 7077892
  7.2 6.0 copy-start.9
  7.2 37.7 %all-reduce.6.cloned.1.call-start = ((), (), s32[]{:S(2)}) async-start(), calls=%async_computation | async-start | bytes 3145728 | tf_op jit(solution)/shard_map/psum | solution.py:146
  7.3 5.9 copy-start.23
  13.2 3.0 copy-start.27
  15.3 2.7 copy-start.2
  15.3 2.7 copy-start.29
  16.2 3.0 copy-start.30
  19.2 2.6 copy-start.49
  19.2 3.2 copy-start.50
  19.2 3.1 copy-start.51
  21.7 59.9 %all-reduce.8.cloned.1.call-start = ((), (), s32[]{:S(2)}) async-start(), calls=%async_computation.1 | async-start | bytes 3145728 | tf_op jit(solution)/shard_map/psum | solution.py:154
  22.3 33.8 %copy-start.45 = (f32[768]{0:T(1024)}, f32[768]{0:T(1024)S(1)}, u32[]{:S(2)}) copy-start(f32[768]{0:T(1024)S(1)} %convert_element_type.138) | copy-start | bytes 9220
  23.0 58.5 %copy-start.31 = (f32[768]{0:T(1024)}, f32[768]{0:T(1024)S(1)}, u32[]{:S(2)}) copy-start(f32[768]{0:T(1024)S(1)} %convert_element_type.137) | copy-start | bytes 9220
  46.6 9.5 %copy-start.3 = (f32[512,768]{1,0:T(8,128)}, f32[512,768]{1,0:T(8,128)S(1)}, u32[]{:S(2)}) copy-start(f32[512,768]{1,0:T(8,128)S(1)} %get-tuple-element.84) | copy-start | bytes 4718596
  46.7 34.9 %copy-start.33 = (f32[512]{0:T(512)}, f32[512]{0:T(512)S(1)}, u32[]{:S(2)}) copy-start(f32[512]{0:T(512)S(1)} %broadcast_multiply_fusion.5) | copy-start | bytes 6148
  47.0 34.6 %copy-start.35 = (f32[512]{0:T(512)}, f32[512]{0:T(512)S(1)}, u32[]{:S(2)}) copy-start(f32[512]{0:T(512)S(1)} %add_rsqrt_fusion.1) | copy-start | bytes 6148
  47.0 10.3 %copy-start.53 = (bf16[1536,768]{1,0:T(8,128)(2,1)S(1)}, bf16[1536,768]{1,0:T(8,128)(2,1)}, u32[]{:S(2)}) copy-start(bf16[1536,768]{1,0:T(8,128)(2,1)} %param.32) | copy-start | bytes 7077892
  57.3 2.8 copy-start.52
  59.8 58.7 %all-reduce.10.cloned.1.call-start = ((), (), s32[]{:S(2)}) async-start(), calls=%async_computation.2 | async-start | bytes 3145728 | tf_op jit(solution)/shard_map/psum | solution.py:169
  81.6 2.9 copy-start.15
  84.5 3.5 copy-start.54
  84.5 3.5 copy-start.56
  88.0 3.3 copy-start.7
  95.0 143.1 %all-reduce.12.cloned.1.call-start = ((), (), s32[]{:S(2)}) async-start(), calls=%async_computation.3 | async-start | bytes 3145728 | tf_op jit(solution)/shard_map/psum | solution.py:204
  101.5 6.0 copy-start.8
  112.6 6.0 copy-start.4
  112.6 6.0 copy-start.32
  112.6 6.0 copy-start.34
  112.6 6.0 copy-start.36
  118.6 6.1 slice-start
  122.0 2.7 slice-start.1
  123.1 12.6 %copy-start.5 = (f32[512,768]{1,0:T(8,128)}, f32[512,768]{1,0:T(8,128)S(1)}, u32[]{:S(2)}) copy-start(f32[512,768]{1,0:T(8,128)S(1)} %get-tuple-element.79) | copy-start | bytes 4718596
  132.1 3.6 copy-start.20
  135.7 3.0 copy-start.26
  140.5 496.4 %all-reduce.14.cloned.1.call-start = ((), (), s32[]{:S(2)}) async-start(), calls=%async_computation.4 | async-start | bytes 28368896 | tf_op jit(solution)/shard_map/psum | solution.py:215
  141.2 4.1 copy-start.12
  143.8 5.3 copy-start.40
  143.8 5.4 copy-start.10
  149.3 12.3 %copy-start.14 = (f32[294912]{0:T(1024)S(1)}, f32[294912]{0:T(1024)}, u32[]{:S(2)}) copy-start(f32[294912]{0:T(1024)} %reshape.201) | copy-start | bytes 3538948
  150.7 34.0 %copy-start.39 = (f32[768]{0:T(1024)S(1)}, f32[768]{0:T(1024)}, u32[]{:S(2)}) copy-start(f32[768]{0:T(1024)} %get-tuple-element.78) | copy-start | bytes 9220
  150.7 35.3 %copy-start.44 = (f32[768]{0:T(1024)S(1)}, f32[768]{0:T(1024)}, u32[]{:S(2)}) copy-start(f32[768]{0:T(1024)} %get-tuple-element.68) | copy-start | bytes 9220
  150.7 36.6 %copy-start.43 = (f32[768]{0:T(1024)S(1)}, f32[768]{0:T(1024)}, u32[]{:S(2)}) copy-start(f32[768]{0:T(1024)} %get-tuple-element.73) | copy-start | bytes 9220
  188.6 4.0 copy-start.48
  193.9 41.0 %copy-start.42 = (f32[768]{0:T(1024)S(1)}, f32[768]{0:T(1024)}, u32[]{:S(2)}) copy-start(f32[768]{0:T(1024)} %get-tuple-element.76) | copy-start | bytes 9220
  193.9 42.3 %copy-start.38 = (f32[768]{0:T(1024)S(1)}, f32[768]{0:T(1024)}, u32[]{:S(2)}) copy-start(f32[768]{0:T(1024)} %get-tuple-element.70) | copy-start | bytes 9220
  193.9 43.6 %copy-start.37 = (f32[768]{0:T(1024)S(1)}, f32[768]{0:T(1024)}, u32[]{:S(2)}) copy-start(f32[768]{0:T(1024)} %get-tuple-element.75) | copy-start | bytes 9220
  659.0 10.1 %copy-start.1 = (bf16[768,1536]{1,0:T(8,128)(2,1)S(1)}, bf16[768,1536]{1,0:T(8,128)(2,1)}, u32[]{:S(2)}) copy-start(bf16[768,1536]{1,0:T(8,128)(2,1)} %param.30) | copy-start | bytes 7077892
  (16 other events, 25.6 us)
Sparse Core Ops, SparseCore 0:
  21.8 23.0 all-reduce.5
  60.0 21.5 all-reduce.7
  95.1 21.5 all-reduce.9
  140.6 21.6 all-reduce.11
  238.2 398.6 all-reduce.13
where the time goes:
time: 682 us; the launch traced here: 676 us
  waiting for transfers between devices  436 us (64%)
  local copies, waits for them, and re-layouts  148 us (22%)
  matrix products  51.4 us (8%)
  other arithmetic  24.9 us (4%)
  between operations  15 us (2%)
    psum x1, waiting for transfers between devices, body(): summed = unflatten(lax.psum(flatten(every), 'dp'), every)  395 us
    unnamed x132, local copies, waits for them, and re-layouts  95.6 us
    slice x10, local copies, waits for them, and re-layouts, unflatten(): pieces.append(flat[offset:offset + count].reshape(grad.shape))  26.4 us
    psum x1, waiting for transfers between devices, body(): attended = lax.psum(matmul(context, out_weight), 'mp')  21.9 us
    psum x1, waiting for transfers between devices, body(): down = lax.psum(matmul(active, down_weight), 'mp')  18.9 us
    dot_general x6, matrix products, matmul(): return jnp.dot(left, right, preferred_element_type=jnp.float32)  17.5 us
    dot_general x6, matrix products, outer_sum(): lax.dot_general(left, right, (((0,), (0,)), ((), ())), preferred_element_...  16.7 us
    reshape x6, local copies, waits for them, and re-layouts, flatten(): return jnp.concatenate([grad.reshape(-1) for grad in grads])  16.1 us
  transfers between devices with their start and end apart: 5, of which 3 were waited for; matrix products, arithmetic and copies ran while one was open for 19% of the time, Pallas kernels for 0%

commit v1 on v0

--- a/solution.py
+++ b/solution.py
@@ -1,6 +1,10 @@
+import functools
+
 import jax
 import jax.numpy as jnp
 from jax import lax
+from jax.experimental import pallas as pl
+from jax.experimental.pallas import tpu as pltpu
 from jax.sharding import PartitionSpec as P
 
 DH = 64
@@ -94,21 +98,134 @@
     )
 
 
-def flatten(grads):
-    return jnp.concatenate([grad.reshape(-1) for grad in grads])
-
-
-def unflatten(flat, grads):
-    pieces = []
-    offset = 0
-    for grad in grads:
-        count = grad.size
-        pieces.append(flat[offset : offset + count].reshape(grad.shape))
-        offset = offset + count
-    return tuple(pieces)
+BLOCK = 384
+CUBE = 16
+
+
+def swap_cores(part):
+    return part + lax.ppermute(part, "mp", [(0, 1), (1, 0)])
+
+
+def hop(block, first, second, ranks):
+    pairs = []
+    for rank in range(ranks):
+        pairs.append((2 * rank, 2 * (rank ^ first)))
+        pairs.append((2 * rank + 1, 2 * (rank ^ second) + 1))
+    return lax.ppermute(block, ("dp", "mp"), pairs)
+
+
+def place():
+    rank = lax.axis_index("dp")
+    core = lax.axis_index("mp")
+    x = rank & 1
+    y = (rank >> 1) & 1
+    z = ((rank >> 2) ^ (rank >> 3)) & 1
+    swapped = core == 1
+    return (jnp.where(swapped, y, x), z, jnp.where(swapped, x, y))
+
+
+def cut_kernel(offsets, left_ref, right_ref, send_ref, keep_ref):
+    for spot in range(8):
+        left = left_ref[:, pl.ds(pl.multiple_of(offsets[spot], 128), BLOCK)]
+        right = right_ref[:, pl.ds(pl.multiple_of(offsets[8 + spot], 128), BLOCK)]
+        product = outer_sum(left, right)
+        if spot < 4:
+            keep_ref[spot] = product
+        else:
+            send_ref[spot - 4] = product
+
+
+def cut_product(left, right, offsets):
+    shape = jax.ShapeDtypeStruct((4, BLOCK, BLOCK), jnp.float32)
+    return pl.pallas_call(
+        cut_kernel,
+        out_shape=(shape, shape),
+        in_specs=[
+            pl.BlockSpec(memory_space=pltpu.SMEM),
+            pl.BlockSpec(memory_space=pltpu.VMEM),
+            pl.BlockSpec(memory_space=pltpu.VMEM),
+        ],
+        out_specs=(pl.BlockSpec(memory_space=pltpu.VMEM), pl.BlockSpec(memory_space=pltpu.VMEM)),
+        compiler_params=pltpu.CompilerParams(vmem_limit_bytes=24 << 20),
+        cost_estimate=pl.CostEstimate(
+            flops=16 * left.shape[0] * BLOCK * BLOCK,
+            bytes_accessed=2 * (left.size + right.size) + 32 * BLOCK * BLOCK,
+            transcendentals=0,
+        ),
+    )(offsets, left, right)
+
+
+def join_kernel(layout, where_ref, near_ref, far_ref, *rest):
+    outs, sem = rest[:-1], rest[-1]
+    copies = []
+    for block in range(8):
+        out, row, column = layout[block]
+        target = outs[out].at[pl.ds(row, BLOCK), pl.ds(column, BLOCK)]
+        spot = where_ref[block]
+        own = where_ref[8 + block]
+
+        @pl.when(own == 0)
+        def _(target=target, spot=spot, block=block):
+            pltpu.make_async_copy(near_ref.at[spot], target, sem.at[block]).start()
+
+        @pl.when(own != 0)
+        def _(target=target, spot=spot, block=block):
+            pltpu.make_async_copy(far_ref.at[spot], target, sem.at[block]).start()
+
+        copies.append(pltpu.make_async_copy(near_ref.at[0], target, sem.at[block]))
+    for copy in copies:
+        copy.wait()
+
+
+def join_blocks(near, far, layout, shapes, where):
+    return pl.pallas_call(
+        functools.partial(join_kernel, layout),
+        out_shape=tuple(jax.ShapeDtypeStruct(shape, jnp.float32) for shape in shapes),
+        in_specs=[
+            pl.BlockSpec(memory_space=pltpu.SMEM),
+            pl.BlockSpec(memory_space=pl.ANY),
+            pl.BlockSpec(memory_space=pl.ANY),
+        ],
+        out_specs=tuple(pl.BlockSpec(memory_space=pl.ANY) for _ in shapes),
+        scratch_shapes=[pltpu.SemaphoreType.DMA((8,))],
+        cost_estimate=pl.CostEstimate(
+            flops=0, bytes_accessed=64 * BLOCK * BLOCK, transcendentals=0
+        ),
+    )(where, near, far)
+
+
+def dp_sum(send, keep, ranks):
+    got = hop(send, 1, 2, ranks)
+    part = keep[2:] + got[2:]
+    low = hop(part, 4, 4, ranks)
+    half = keep[1] + got[1] + low[1]
+    quarter = hop(half, 2, 1, ranks)
+    own = keep[0] + got[0] + low[0] + quarter
+    total = own + hop(own, 12, 12, ranks)
+    bit = CUBE
+    while bit < ranks:
+        total = total + hop(total, bit, bit, ranks)
+        bit = 2 * bit
+    other = hop(total, 2, 1, ranks)
+    pair = jnp.stack([total, other])
+    rest = hop(pair, 4, 4, ranks)
+    near = jnp.concatenate([pair, rest])
+    far = hop(near, 1, 2, ranks)
+    return near, far
+
+
+def dp_sum_small(value, ranks):
+    for bit in (1, 2, 4, 12):
+        value = value + hop(value, bit, bit, ranks)
+    bit = CUBE
+    while bit < ranks:
+        value = value + hop(value, bit, bit, ranks)
+        bit = 2 * bit
+    return value
 
 
 def body(
+    ranks,
     tokens,
     lengths,
     cotangent,
@@ -128,6 +245,15 @@
     final_gain,
     final_shift,
 ):
+    first, second, third = place()
+    mine = 4 * first + 2 * second + third
+    spots = jnp.arange(8, dtype=jnp.int32)
+    blocks = spots ^ mine
+    rows_of = (blocks >> 1) * BLOCK
+    columns_of = (blocks & 1) * BLOCK
+    rest_left = jnp.where(blocks < 6, (blocks & 1) * BLOCK, 2 * BLOCK)
+    rest_right = jnp.where(blocks < 6, (blocks >> 1) * BLOCK, (blocks - 3) * BLOCK)
+    where = jnp.concatenate([blocks & 3, blocks >> 2]).astype(jnp.int32)
     rows = tokens.shape[0]
     pages = lengths.shape[0]
     length = rows // pages
@@ -143,7 +269,7 @@
         attend_page, (by_page(query), by_page(keys), by_page(values), lengths)
     )
     context = context.reshape(rows, heads * DH)
-    attended = lax.psum(matmul(context, out_weight), "mp")
+    attended = swap_cores(matmul(context, out_weight))
     inputs = tokens.astype(jnp.float32)
     middle, mid_normal, mid_scale = norm_forward(
         inputs + attended + out_bias.astype(jnp.float32), mid_gain, mid_shift
@@ -151,7 +277,7 @@
     mid_low = middle.astype(jnp.bfloat16)
     before = matmul(mid_low, up_weight) + up_bias.astype(jnp.float32)
     active = jax.nn.gelu(before, approximate=False).astype(jnp.bfloat16)
-    down = lax.psum(matmul(active, down_weight), "mp")
+    down = swap_cores(matmul(active, down_weight))
     result, final_normal, final_scale = norm_forward(
         middle + down + down_bias.astype(jnp.float32), final_gain, final_shift
     )
@@ -162,19 +288,93 @@
     )
     down_bias_grad = jnp.sum(second_grad, axis=0)
     second_low = second_grad.astype(jnp.bfloat16)
-    down_weight_grad = outer_sum(active, second_low)
+    down_cut = cut_product(active, second_low, jnp.concatenate([rows_of, columns_of]))
     before_grad = (matmul_flip(second_low, down_weight) * gelu_slope(before)).astype(jnp.bfloat16)
-    up_weight_grad = outer_sum(mid_low, before_grad)
+    up_cut = cut_product(mid_low, before_grad, jnp.concatenate([columns_of, rows_of]))
     up_bias_grad = jnp.sum(before_grad.astype(jnp.float32), axis=0)
-    mid_grad = second_grad + lax.psum(matmul_flip(before_grad, up_weight), "mp")
+    mid_grad = second_grad + swap_cores(matmul_flip(before_grad, up_weight))
     first_grad, mid_gain_grad, mid_shift_grad = norm_backward(
         mid_grad, mid_normal, mid_scale, mid_gain
     )
     out_bias_grad = jnp.sum(first_grad, axis=0)
     first_low = first_grad.astype(jnp.bfloat16)
-    out_weight_grad = outer_sum(context, first_low)
     context_grad = matmul_flip(first_low, out_weight).astype(jnp.bfloat16)
-    ffn_grads = (
+    query_grad, key_grad, value_grad = lax.map(
+        attend_back,
+        (by_page(query), by_page(keys), by_page(values), lengths, log_total, by_page(context_grad)),
+    )
+    query_grad = query_grad.reshape(rows, heads * DH)
+    key_grad = key_grad.reshape(rows, heads * DH)
+    value_grad = value_grad.reshape(rows, heads * DH)
+    rest_cut = cut_product(
+        jnp.concatenate([tokens, context], axis=1),
+        jnp.concatenate([query_grad, key_grad, value_grad, first_low], axis=1),
+        jnp.concatenate([rest_left, rest_right]),
+    )
+    query_bias_grad = jnp.sum(query_grad.astype(jnp.float32), axis=0)
+    value_bias_grad = jnp.sum(value_grad.astype(jnp.float32), axis=0)
+    input_part = (
+        matmul_flip(query_grad, query_weight)
+        + matmul_flip(key_grad, key_weight)
+        + matmul_flip(value_grad, value_weight)
+    )
+    input_grad = (first_grad + swap_cores(input_part)).astype(jnp.bfloat16)
+    small = jnp.concatenate(
+        [
+            query_bias_grad,
+            value_bias_grad,
+            up_bias_grad,
+            out_bias_grad,
+            mid_gain_grad,
+            mid_shift_grad,
+            down_bias_grad,
+            final_gain_grad,
+            final_shift_grad,
+        ]
+    ).reshape(-1, 384)
+    small = dp_sum_small(small, ranks).reshape(-1)
+    edges = [0, 384, 768, 2304, 3072, 3840, 4608, 5376, 6144, 6912]
+    (
+        query_bias_grad,
+        value_bias_grad,
+        up_bias_grad,
+        out_bias_grad,
+        mid_gain_grad,
+        mid_shift_grad,
+        down_bias_grad,
+        final_gain_grad,
+        final_shift_grad,
+    ) = [small[low:high] for low, high in zip(edges[:-1], edges[1:])]
+    width = tokens.shape[1]
+    hidden = up_weight.shape[1]
+    down_layout = [(0, (block >> 1) * BLOCK, (block & 1) * BLOCK) for block in range(8)]
+    up_layout = [(0, (block & 1) * BLOCK, (block >> 1) * BLOCK) for block in range(8)]
+    rest_layout = [(block >> 1, (block & 1) * BLOCK, 0) for block in range(6)] + [
+        (3, 0, 0),
+        (3, 0, BLOCK),
+    ]
+    (down_weight_grad,) = join_blocks(
+        *dp_sum(*down_cut, ranks), down_layout, [(hidden, width)], where
+    )
+    (up_weight_grad,) = join_blocks(
+        *dp_sum(*up_cut, ranks), up_layout, [(width, hidden)], where
+    )
+    query_weight_grad, key_weight_grad, value_weight_grad, out_weight_grad = join_blocks(
+        *dp_sum(*rest_cut, ranks),
+        rest_layout,
+        [(width, heads * DH)] * 3 + [(heads * DH, width)],
+        where,
+    )
+    return (
+        layer_out,
+        input_grad,
+        query_weight_grad,
+        query_bias_grad,
+        key_weight_grad,
+        value_weight_grad,
+        value_bias_grad,
+        out_weight_grad,
+        out_bias_grad,
         mid_gain_grad,
         mid_shift_grad,
         up_weight_grad,
@@ -184,54 +384,6 @@
         final_gain_grad,
         final_shift_grad,
     )
-    query_grad, key_grad, value_grad = lax.map(
-        attend_back,
-        (by_page(query), by_page(keys), by_page(values), lengths, log_total, by_page(context_grad)),
-    )
-    query_grad = query_grad.reshape(rows, heads * DH)
-    key_grad = key_grad.reshape(rows, heads * DH)
-    value_grad = value_grad.reshape(rows, heads * DH)
-    query_weight_grad = outer_sum(tokens, query_grad)
-    query_bias_grad = jnp.sum(query_grad.astype(jnp.float32), axis=0)
-    key_weight_grad = outer_sum(tokens, key_grad)
-    value_weight_grad = outer_sum(tokens, value_grad)
-    value_bias_grad = jnp.sum(value_grad.astype(jnp.float32), axis=0)
-    input_part = (
-        matmul_flip(query_grad, query_weight)
-        + matmul_flip(key_grad, key_weight)
-        + matmul_flip(value_grad, value_weight)
-    )
-    input_grad = (first_grad + lax.psum(input_part, "mp")).astype(jnp.bfloat16)
-    attn_grads = (
-        query_weight_grad,
-        query_bias_grad,
-        key_weight_grad,
-        value_weight_grad,
-        value_bias_grad,
-        out_weight_grad,
-        out_bias_grad,
-    )
-    every = attn_grads + ffn_grads
-    summed = unflatten(lax.psum(flatten(every), "dp"), every)
-    return (
-        layer_out,
-        input_grad,
-        summed[0],
-        summed[1],
-        summed[2],
-        summed[3],
-        summed[4],
-        summed[5],
-        summed[6],
-        summed[7],
-        summed[8],
-        summed[9],
-        summed[10],
-        summed[11],
-        summed[12],
-        summed[13],
-        summed[14],
-    )
 
 
 def solution(mesh):
@@ -274,4 +426,4 @@
         P(),
         P(),
     )
-    return jax.shard_map(body, mesh=mesh, in_specs=in_specs, out_specs=out_specs, check_vma=False)
+    return jax.shard_map(functools.partial(body, mesh.shape["dp"]), mesh=mesh, in_specs=in_specs, out_specs=out_specs, check_vma=False)

time: 682 us -> 818 us (1.20)
  Pallas kernels: 0 us -> 444 us
  waiting for transfers between devices: 436 us -> 194 us
  local copies, waits for them, and re-layouts: 148 us -> 18.2 us
  starting transfers between devices: 0.61 us -> 80.4 us
  other arithmetic: 24.9 us -> 42.2 us
  matrix products: 51.4 us -> 35.8 us
  between operations: 15 us -> 2.42 us
    pallas_call x0 -> x6, Pallas kernels: none -> 444 us  [the longest x3 434 us: join_blocks(): pl.pallas_call(functools.partial(join_kernel, layout), out_shape=tuple((j...]
    psum x5 -> x0, waiting for transfers between devices: 436 us -> none  [the longest x1 395 us: body(): summed = unflatten(lax.psum(flatten(every), 'dp'), every)]
    ppermute x0 -> x29, waiting for transfers between devices: none -> 194 us  [the longest x25 188 us: hop(): return lax.ppermute(block, ('dp', 'mp'), pairs)]
    unnamed x132 -> x122, local copies, waits for them, and re-layouts: 95.6 us -> 6.52 us
    ppermute x0 -> x29, starting transfers between devices: none -> 80.4 us  [the longest x25 79.1 us: hop(): return lax.ppermute(block, ('dp', 'mp'), pairs)]
    slice x10, local copies, waits for them, and re-layouts: 26.4 us -> 4.82 us  [body(): small[low:high]]
    dot_general x6 -> x0, matrix products: 16.7 us -> none  [outer_sum(): lax.dot_general(left, right, (((0,), (0,)), ((), ())), preferred_element_...]
    reshape x7 -> x5, local copies, waits for them, and re-layouts: 21.8 us -> 6.69 us  [the longest x1 1.91 us: body(): value_grad = value_grad.reshape(rows, heads * DH)]
  transfers between devices with their start and end apart: 5 -> 29, of which waited for: 3 -> 17; matrix products, arithmetic and copies ran while one was open for 19% -> 7% of each run, Pallas kernels for 0% -> 37%
where the time goes in v1:
time: 818 us; the launch traced here: 817 us
  Pallas kernels  444 us (54%)
  waiting for transfers between devices  194 us (24%)
  starting transfers between devices  80.4 us (10%)
  other arithmetic  42.2 us (5%)
  matrix products  35.8 us (4%)
  local copies, waits for them, and re-layouts  18.2 us (2%)
    pallas_call x3, Pallas kernels, join_blocks(): pl.pallas_call(functools.partial(join_kernel, layout), out_shape=tuple((j...  434 us
    ppermute x25, waiting for transfers between devices, hop(): return lax.ppermute(block, ('dp', 'mp'), pairs)  188 us
    ppermute x25, starting transfers between devices, hop(): return lax.ppermute(block, ('dp', 'mp'), pairs)  79.1 us
  transfers between devices with their start and end apart: 29, of which 17 were waited for; matrix products, arithmetic and copies ran while one was open for 7% of the time, Pallas kernels for 37%

profile of v1, /device:TPU:0, one launch (start us, length us, event | category | flops | bytes accessed | tf_op | source)
XLA Modules:
  0.0 817.1 jit_solution(15055552308701200925)
XLA Ops:
  4.8 2.0 fusion.31
  14.0 3.0 collective-permute-done
  18.1 8.6 %fusion.7 = (bf16[512,1536]{1,0:T(8,128)(2,1)S(1)}, f32[512,1536]{1,0:T(8,128)S(1)}) fusion(f32[1536]{0:T(1024)S(1)} %convert_element_type.140, bf16[512,768]{1,0:T(8,128)(2,1)S(1)} %fusion.30.left_ref, bf16[768,1536]{1,0:T(8,128)(2,1)S(1)} %copy-done), kind=kOutput, calls=%fused_computation.17 | convolution fusion | flops 1259864064 | bytes 7870464 | tf_op jit(solution)/shard_map/dot_general | solution.py:20
  28.6 3.0 collective-permute-done.1
  34.0 2.1 fusion.50
  37.3 2.8 convert_reduce_fusion
  40.1 2.6 fusion.59
  45.6 3.8 shard_map.307
  49.4 2.6 collective-permute-start.15
  52.0 3.8 shard_map.309
  55.8 3.3 multiply_reduce_fusion
  71.6 1.9 copy.52
  73.6 1.9 copy.51
  75.5 3.4 convert_reduce_fusion.3
  78.9 1.9 copy.50
  82.7 2.4 shard_map.305
  85.1 2.1 collective-permute-start.4
  90.2 14.2 %collective-permute-done.22 = f32[4,384,384]{2,1,0:T(8,128)} collective-permute-done((f32[4,384,384]{2,1,0:T(8,128)}, f32[4,384,384]{2,1,0:T(8,128)}, u32[]{:S(2)}, u32[]{:S(2)}) %collective-permute-start.22) | collective-permute-done | bytes 2359328 | tf_op jit(solution)/shard_map/ppermute | solution.py:114
  105.8 2.2 collective-permute-start.23
  108.0 21.6 %collective-permute-done.4 = f32[4,384,384]{2,1,0:T(8,128)S(1)} collective-permute-done((f32[4,384,384]{2,1,0:T(8,128)S(1)}, f32[4,384,384]{2,1,0:T(8,128)S(1)}, u32[]{:S(2)}, u32[]{:S(2)}) %collective-permute-start.4) | collective-permute-done | bytes 2359328 | tf_op jit(solution)/shard_map/ppermute | solution.py:114
  129.8 2.2 collective-permute-start.5
  134.7 8.1 collective-permute-done.23
  145.6 21.1 %collective-permute-done.5 = f32[2,384,384]{2,1,0:T(8,128)S(1)} collective-permute-done((f32[2,384,384]{2,1,0:T(8,128)S(1)}, f32[2,384,384]{2,1,0:T(8,128)S(1)}, u32[]{:S(2)}, u32[]{:S(2)}) %collective-permute-start.5) | collective-permute-done | bytes 1179680 | tf_op jit(solution)/shard_map/ppermute | solution.py:114
  168.3 3.8 collective-permute-start.18
  173.5 3.2 collective-permute-done.6
  176.9 3.7 collective-permute-start.7
  180.5 6.0 collective-permute-done.18
  188.4 10.8 %collective-permute-done.25 = f32[384,384]{1,0:T(8,128)S(1)} collective-permute-done((f32[384,384]{1,0:T(8,128)S(1)}, f32[384,384]{1,0:T(8,128)S(1)}, u32[]{:S(2)}, u32[]{:S(2)}) %collective-permute-start.25) | collective-permute-done | bytes 589856 | tf_op jit(solution)/shard_map/ppermute | solution.py:114
  201.0 10.8 %collective-permute-done.7 = f32[384,384]{1,0:T(8,128)S(1)} collective-permute-done((f32[384,384]{1,0:T(8,128)S(1)}, f32[384,384]{1,0:T(8,128)S(1)}, u32[]{:S(2)}, u32[]{:S(2)}) %collective-permute-start.7) | collective-permute-done | bytes 589856 | tf_op jit(solution)/shard_map/ppermute | solution.py:114
  213.1 37.2 %collective-permute-start.20 = (f32[2,384,384]{2,1,0:T(8,128)}, f32[2,384,384]{2,1,0:T(8,128)}, u32[]{:S(2)}, u32[]{:S(2)}) collective-permute-start(f32[2,384,384]{2,1,0:T(8,128)} %pad_maximum_fusion.6), channel_id=1, source_target_pairs={{0,8},{1,9},{2,10},{3,11},{4,12},{5,13},{6,14},{7,15},{8,0},{9,1},... | collective-permute-start | bytes 3538952 | tf_op jit(solution)/shard_map/ppermute | solution.py:114
  252.6 7.5 collective-permute-start.9
  262.5 15.0 %collective-permute-done.20 = f32[2,384,384]{2,1,0:T(8,128)} collective-permute-done((f32[2,384,384]{2,1,0:T(8,128)}, f32[2,384,384]{2,1,0:T(8,128)}, u32[]{:S(2)}, u32[]{:S(2)}) %collective-permute-start.20) | collective-permute-done | bytes 1179680 | tf_op jit(solution)/shard_map/ppermute | solution.py:114
  277.5 2.8 pad_maximum_fusion.1.near_ref
  280.3 22.4 %collective-permute-done.27 = f32[2,384,384]{2,1,0:T(8,128)} collective-permute-done((f32[2,384,384]{2,1,0:T(8,128)}, f32[2,384,384]{2,1,0:T(8,128)}, u32[]{:S(2)}, u32[]{:S(2)}) %collective-permute-start.27) | collective-permute-done | bytes 1179680 | tf_op jit(solution)/shard_map/ppermute | solution.py:114
  302.8 2.9 pad_maximum_fusion.2.near_ref
  305.7 21.3 %collective-permute-done.9 = f32[2,384,384]{2,1,0:T(8,128)} collective-permute-done((f32[2,384,384]{2,1,0:T(8,128)}, f32[2,384,384]{2,1,0:T(8,128)}, u32[]{:S(2)}, u32[]{:S(2)}) %collective-permute-start.9) | collective-permute-done | bytes 1179680 | tf_op jit(solution)/shard_map/ppermute | solution.py:114
  327.0 2.9 pad_maximum_fusion.near_ref
  334.2 26.6 %collective-permute-done.11 = f32[18,384]{1,0:T(8,128)S(1)} collective-permute-done((f32[18,384]{1,0:T(8,128)S(1)}, f32[18,384]{1,0:T(8,128)S(1)}, u32[]{:S(2)}, u32[]{:S(2)}) %collective-permute-start.11) | collective-permute-done | bytes 27680 | tf_op jit(solution)/shard_map/ppermute | solution.py:114
  360.8 2.0 collective-permute-start.12
  362.8 1.9 collective-permute-done.12
  364.8 2.0 collective-permute-start.13
  366.8 1.9 collective-permute-done.13
  368.8 2.5 collective-permute-start.14
  371.8 2.7 collective-permute-done.14
  379.4 3.0 add_convert_fusion
  382.4 144.8 %shard_map.308 = f32[768,1536]{1,0:T(8,128)} custom-call(s32[16]{0:T(128)} %pad_add_fusion.where_ref, f32[4,384,384]{2,1,0:T(8,128)} %pad_maximum_fusion.1.near_ref, f32[4,384,384]{2,1,0:T(8,128)} %collective-permute-done.21.far_ref), custom_call_target="tpu_custom_call" | custom-call | bytes 9437184 | tf_op jit(solution)/shard_map/pallas_call | solution.py:181
  527.2 144.9 %shard_map.310 = f32[1536,768]{1,0:T(8,128)} custom-call(s32[16]{0:T(128)} %pad_add_fusion.where_ref, f32[4,384,384]{2,1,0:T(8,128)} %pad_maximum_fusion.2.near_ref, f32[4,384,384]{2,1,0:T(8,128)} %collective-permute-done.28.far_ref), custom_call_target="tpu_custom_call" | custom-call | bytes 9437184 | tf_op jit(solution)/shard_map/pallas_call | solution.py:181
  672.1 144.8 %shard_map.306 = (f32[768,384]{1,0:T(8,128)}, f32[768,384]{1,0:T(8,128)}, f32[768,384]{1,0:T(8,128)}, f32[384,768]{1,0:T(8,128)}) custom-call(s32[16]{0:T(128)} %pad_add_fusion.where_ref, f32[4,384,384]{2,1,0:T(8,128)} %pad_maximum_fusion.near_ref, f32[4,384,384]{2,1,0:T(8,128)} %collective-permute-done.10.far_ref), custom_call_target="tpu_custom_call" | custom-call | bytes 9437184 | tf_op jit(solution)/shard_map/pallas_call | solution.py:181
  (239 shorter events, 66.6 us)
Async XLA Ops:
  0.7 17.4 %copy-start = (bf16[768,1536]{1,0:T(8,128)(2,1)S(1)}, bf16[768,1536]{1,0:T(8,128)(2,1)}, u32[]{:S(2)}) copy-start(bf16[768,1536]{1,0:T(8,128)(2,1)} %param.30) | copy-start | bytes 7077892
  0.7 6.1 copy-start.24
  13.4 3.6 collective-permute-start
  17.4 14.3 %copy-start.13 = (f32[512,768]{1,0:T(8,128)}, f32[512,768]{1,0:T(8,128)S(1)}, u32[]{:S(2)}) copy-start(f32[512,768]{1,0:T(8,128)S(1)} %get-tuple-element.106) | copy-start | bytes 4718596
  18.1 8.6 %copy-start.4 = (bf16[512,768]{1,0:T(8,128)(2,1)}, bf16[512,768]{1,0:T(8,128)(2,1)S(1)}, u32[]{:S(2)}) copy-start(bf16[512,768]{1,0:T(8,128)(2,1)S(1)} %fusion.30.left_ref) | copy-start | bytes 2359300
  18.1 8.7 %copy-start.54 = (bf16[1536,768]{1,0:T(8,128)(2,1)S(1)}, bf16[1536,768]{1,0:T(8,128)(2,1)}, u32[]{:S(2)}) copy-start(bf16[1536,768]{1,0:T(8,128)(2,1)} %param.32) | copy-start | bytes 7077892
  28.2 3.5 collective-permute-start.1
  42.7 13.1 %collective-permute-start.2 = (f32[512,768]{1,0:T(8,128)}, f32[512,768]{1,0:T(8,128)}, u32[]{:S(2)}, u32[]{:S(2)}) collective-permute-start(f32[512,768]{1,0:T(8,128)} %fusion.59), channel_id=1, source_target_pairs={{0,1},{1,0},{2,3},{3,2},{4,5},{5,4},{6,7},{7,6},{8,9},{9,8},{10,11... | collective-permute-start | bytes 4718600 | tf_op jit(solution)/shard_map/ppermute | solution.py:106
  45.6 6.5 copy-start.7
  45.6 6.4 copy-start.9
  49.4 9.7 %copy-start.2 = (f32[4,384,384]{2,1,0:T(8,128)}, f32[4,384,384]{2,1,0:T(8,128)S(1)}, u32[]{:S(2)}) copy-start(f32[4,384,384]{2,1,0:T(8,128)S(1)} %get-tuple-element.84) | copy-start | bytes 7077892
  49.4 6.5 copy-start.14
  49.4 6.5 copy-start.17
  49.4 37.8 %collective-permute-start.15 = (f32[4,384,384]{2,1,0:T(8,128)}, f32[4,384,384]{2,1,0:T(8,128)}, u32[]{:S(2)}, u32[]{:S(2)}) collective-permute-start(f32[4,384,384]{2,1,0:T(8,128)} %get-tuple-element.85), channel_id=1, source_target_pairs={{0,2},{1,5},{2,0},{3,7},{4,6},{5,1},{6,4},{7,3},{8,10},{9,13},{10,... | collective-permute-start | bytes 7077896 | tf_op jit(solution)/shard_map/ppermute | solution.py:114
  55.8 48.6 %collective-permute-start.22 = (f32[4,384,384]{2,1,0:T(8,128)}, f32[4,384,384]{2,1,0:T(8,128)}, u32[]{:S(2)}, u32[]{:S(2)}) collective-permute-start(f32[4,384,384]{2,1,0:T(8,128)} %get-tuple-element.87), channel_id=1, source_target_pairs={{0,2},{1,5},{2,0},{3,7},{4,6},{5,1},{6,4},{7,3},{8,10},{9,13},{10,... | collective-permute-start | bytes 7077896 | tf_op jit(solution)/shard_map/ppermute | solution.py:114
  85.1 44.5 %collective-permute-start.4 = (f32[4,384,384]{2,1,0:T(8,128)S(1)}, f32[4,384,384]{2,1,0:T(8,128)S(1)}, u32[]{:S(2)}, u32[]{:S(2)}) collective-permute-start(f32[4,384,384]{2,1,0:T(8,128)S(1)} %get-tuple-element.79), channel_id=1, source_target_pairs={{0,2},{1,5},{2,0},{3,7},{4,6},{5,1},{6,4},{7,3},{8,10},{9,13},{10,... | collective-permute-start | bytes 7077896 | tf_op jit(solution)/shard_map/ppermute | solution.py:114
  88.6 43.4 %collective-permute-start.16 = (f32[2,384,384]{2,1,0:T(8,128)S(1)}, f32[2,384,384]{2,1,0:T(8,128)S(1)}, u32[]{:S(2)}, u32[]{:S(2)}) collective-permute-start(f32[2,384,384]{2,1,0:T(8,128)S(1)} %slice_add_fusion.1), channel_id=1, source_target_pairs={{0,8},{1,9},{2,10},{3,11},{4,12},{5,13},{6,14},{7,15},{8,0},{9,1},... | collective-permute-start | bytes 3538952 | tf_op jit(solution)/shard_map/ppermute | solution.py:114
  105.8 37.0 %collective-permute-start.23 = (f32[2,384,384]{2,1,0:T(8,128)S(1)}, f32[2,384,384]{2,1,0:T(8,128)S(1)}, u32[]{:S(2)}, u32[]{:S(2)}) collective-permute-start(f32[2,384,384]{2,1,0:T(8,128)S(1)} %slice_add_fusion), channel_id=1, source_target_pairs={{0,8},{1,9},{2,10},{3,11},{4,12},{5,13},{6,14},{7,15},{8,0},{9,1},... | collective-permute-start | bytes 3538952 | tf_op jit(solution)/shard_map/ppermute | solution.py:114
  129.8 36.9 %collective-permute-start.5 = (f32[2,384,384]{2,1,0:T(8,128)S(1)}, f32[2,384,384]{2,1,0:T(8,128)S(1)}, u32[]{:S(2)}, u32[]{:S(2)}) collective-permute-start(f32[2,384,384]{2,1,0:T(8,128)S(1)} %slice_add_fusion.2), channel_id=1, source_target_pairs={{0,8},{1,9},{2,10},{3,11},{4,12},{5,13},{6,14},{7,15},{8,0},{9,1},... | collective-permute-start | bytes 3538952 | tf_op jit(solution)/shard_map/ppermute | solution.py:114
  133.1 34.0 %collective-permute-start.17 = (f32[384,384]{1,0:T(8,128)S(1)}, f32[384,384]{1,0:T(8,128)S(1)}, u32[]{:S(2)}, u32[]{:S(2)}) collective-permute-start(f32[384,384]{1,0:T(8,128)S(1)} %fusion.42), channel_id=1, source_target_pairs={{0,4},{1,3},{2,6},{3,1},{4,0},{5,7},{6,2},{7,5},{8,12},{9,11},{10,... | collective-permute-start | bytes 1769480 | tf_op jit(solution)/shard_map/ppermute | solution.py:114
  144.0 28.2 %collective-permute-start.24 = (f32[384,384]{1,0:T(8,128)S(1)}, f32[384,384]{1,0:T(8,128)S(1)}, u32[]{:S(2)}, u32[]{:S(2)}) collective-permute-start(f32[384,384]{1,0:T(8,128)S(1)} %fusion.39), channel_id=1, source_target_pairs={{0,4},{1,3},{2,6},{3,1},{4,0},{5,7},{6,2},{7,5},{8,12},{9,11},{10,... | collective-permute-start | bytes 1769480 | tf_op jit(solution)/shard_map/ppermute | solution.py:114
  166.7 9.9 %collective-permute-start.6 = (f32[384,384]{1,0:T(8,128)S(1)}, f32[384,384]{1,0:T(8,128)S(1)}, u32[]{:S(2)}, u32[]{:S(2)}) collective-permute-start(f32[384,384]{1,0:T(8,128)S(1)} %fusion.45), channel_id=1, source_target_pairs={{0,4},{1,3},{2,6},{3,1},{4,0},{5,7},{6,2},{7,5},{8,12},{9,11},{10,... | collective-permute-start | bytes 1769480 | tf_op jit(solution)/shard_map/ppermute | solution.py:114
  168.3 18.2 %collective-permute-start.18 = (f32[384,384]{1,0:T(8,128)S(1)}, f32[384,384]{1,0:T(8,128)S(1)}, u32[]{:S(2)}, u32[]{:S(2)}) collective-permute-start(f32[384,384]{1,0:T(8,128)S(1)} %fusion.44), channel_id=1, source_target_pairs={{0,24},{1,25},{2,26},{3,27},{4,28},{5,29},{6,30},{7,31},{8,16},{9,... | collective-permute-start | bytes 1769480 | tf_op jit(solution)/shard_map/ppermute | solution.py:114
  173.3 25.8 %collective-permute-start.25 = (f32[384,384]{1,0:T(8,128)S(1)}, f32[384,384]{1,0:T(8,128)S(1)}, u32[]{:S(2)}, u32[]{:S(2)}) collective-permute-start(f32[384,384]{1,0:T(8,128)S(1)} %fusion.41), channel_id=1, source_target_pairs={{0,24},{1,25},{2,26},{3,27},{4,28},{5,29},{6,30},{7,31},{8,16},{9,... | collective-permute-start | bytes 1769480 | tf_op jit(solution)/shard_map/ppermute | solution.py:114
  176.9 34.9 %collective-permute-start.7 = (f32[384,384]{1,0:T(8,128)S(1)}, f32[384,384]{1,0:T(8,128)S(1)}, u32[]{:S(2)}, u32[]{:S(2)}) collective-permute-start(f32[384,384]{1,0:T(8,128)S(1)} %fusion.47), channel_id=1, source_target_pairs={{0,24},{1,25},{2,26},{3,27},{4,28},{5,29},{6,30},{7,31},{8,16},{9,... | collective-permute-start | bytes 1769480 | tf_op jit(solution)/shard_map/ppermute | solution.py:114
  186.6 25.3 %collective-permute-start.19 = (f32[384,384]{1,0:T(8,128)S(1)}, f32[384,384]{1,0:T(8,128)S(1)}, u32[]{:S(2)}, u32[]{:S(2)}) collective-permute-start(f32[384,384]{1,0:T(8,128)S(1)} %add.279), channel_id=1, source_target_pairs={{0,4},{1,3},{2,6},{3,1},{4,0},{5,7},{6,2},{7,5},{8,12},{9,11},{10,... | collective-permute-start | bytes 1769480 | tf_op jit(solution)/shard_map/ppermute | solution.py:114
  199.2 51.2 %collective-permute-start.26 = (f32[384,384]{1,0:T(8,128)S(1)}, f32[384,384]{1,0:T(8,128)S(1)}, u32[]{:S(2)}, u32[]{:S(2)}) collective-permute-start(f32[384,384]{1,0:T(8,128)S(1)} %add.288), channel_id=1, source_target_pairs={{0,4},{1,3},{2,6},{3,1},{4,0},{5,7},{6,2},{7,5},{8,12},{9,11},{10,... | collective-permute-start | bytes 1769480 | tf_op jit(solution)/shard_map/ppermute | solution.py:114
  211.8 39.6 %collective-permute-start.8 = (f32[384,384]{1,0:T(8,128)S(1)}, f32[384,384]{1,0:T(8,128)S(1)}, u32[]{:S(2)}, u32[]{:S(2)}) collective-permute-start(f32[384,384]{1,0:T(8,128)S(1)} %add.266), channel_id=1, source_target_pairs={{0,4},{1,3},{2,6},{3,1},{4,0},{5,7},{6,2},{7,5},{8,12},{9,11},{10,... | collective-permute-start | bytes 1769480 | tf_op jit(solution)/shard_map/ppermute | solution.py:114
  211.9 38.4 %copy-start.28 = (f32[384,384]{1,0:T(8,128)}, f32[384,384]{1,0:T(8,128)S(1)}, u32[]{:S(2)}) copy-start(f32[384,384]{1,0:T(8,128)S(1)} %collective-permute-done.19) | copy-start | bytes 1769476
  213.1 64.4 %collective-permute-start.20 = (f32[2,384,384]{2,1,0:T(8,128)}, f32[2,384,384]{2,1,0:T(8,128)}, u32[]{:S(2)}, u32[]{:S(2)}) collective-permute-start(f32[2,384,384]{2,1,0:T(8,128)} %pad_maximum_fusion.6), channel_id=1, source_target_pairs={{0,8},{1,9},{2,10},{3,11},{4,12},{5,13},{6,14},{7,15},{8,0},{9,1},... | collective-permute-start | bytes 3538952 | tf_op jit(solution)/shard_map/ppermute | solution.py:114
  250.4 9.8 %copy-start.21 = (bf16[6,64,512]{2,1,0:T(8,128)(2,1)S(1)}, bf16[6,64,512]{2,1,0:T(8,128)(2,1)}, u32[]{:S(2)}) copy-start(bf16[6,64,512]{2,1,0:T(8,128)(2,1)} %get-tuple-element.121) | copy-start | bytes 1179652
  251.5 51.3 %collective-permute-start.27 = (f32[2,384,384]{2,1,0:T(8,128)}, f32[2,384,384]{2,1,0:T(8,128)}, u32[]{:S(2)}, u32[]{:S(2)}) collective-permute-start(f32[2,384,384]{2,1,0:T(8,128)} %pad_maximum_fusion.7), channel_id=1, source_target_pairs={{0,8},{1,9},{2,10},{3,11},{4,12},{5,13},{6,14},{7,15},{8,0},{9,1},... | collective-permute-start | bytes 3538952 | tf_op jit(solution)/shard_map/ppermute | solution.py:114
  251.5 10.4 %copy-start.22 = (bf16[6,64,512]{2,1,0:T(8,128)(2,1)S(1)}, bf16[6,64,512]{2,1,0:T(8,128)(2,1)}, u32[]{:S(2)}) copy-start(bf16[6,64,512]{2,1,0:T(8,128)(2,1)} %fusion.34) | copy-start | bytes 1179652
  252.6 74.4 %collective-permute-start.9 = (f32[2,384,384]{2,1,0:T(8,128)}, f32[2,384,384]{2,1,0:T(8,128)}, u32[]{:S(2)}, u32[]{:S(2)}) collective-permute-start(f32[2,384,384]{2,1,0:T(8,128)} %pad_maximum_fusion.5), channel_id=1, source_target_pairs={{0,8},{1,9},{2,10},{3,11},{4,12},{5,13},{6,14},{7,15},{8,0},{9,1},... | collective-permute-start | bytes 3538952 | tf_op jit(solution)/shard_map/ppermute | solution.py:114
  260.1 17.4 %copy-start.29 = (f32[384,384]{1,0:T(8,128)S(1)}, f32[384,384]{1,0:T(8,128)}, u32[]{:S(2)}) copy-start(f32[384,384]{1,0:T(8,128)} %copy-done.28) | copy-start | bytes 1769476
  262.5 40.2 %copy-start.27 = (f32[384,384]{1,0:T(8,128)S(1)}, f32[384,384]{1,0:T(8,128)}, u32[]{:S(2)}) copy-start(f32[384,384]{1,0:T(8,128)} %copy-done.26) | copy-start | bytes 1769476
  280.3 102.1 %collective-permute-start.21 = (f32[4,384,384]{2,1,0:T(8,128)}, f32[4,384,384]{2,1,0:T(8,128)}, u32[]{:S(2)}, u32[]{:S(2)}) collective-permute-start(f32[4,384,384]{2,1,0:T(8,128)} %pad_maximum_fusion.1.near_ref), channel_id=1, source_target_pairs={{0,2},{1,5},{2,0},{3,7},{4,6},{5,1},{6,4},{7,3},{8,10},{9,13},{10,... | collective-permute-start | bytes 7077896 | tf_op jit(solution)/shard_map/ppermute | solution.py:114
  305.6 25.4 %copy-start.20 = (bf16[6,64,512]{2,1,0:T(8,128)(2,1)S(1)}, bf16[6,64,512]{2,1,0:T(8,128)(2,1)}, u32[]{:S(2)}) copy-start(bf16[6,64,512]{2,1,0:T(8,128)(2,1)} %get-tuple-element.123) | copy-start | bytes 1179652
  305.7 25.4 %copy-start.37 = (bf16[768,384]{1,0:T(8,128)(2,1)S(1)}, bf16[768,384]{1,0:T(8,128)(2,1)}, u32[]{:S(2)}) copy-start(bf16[768,384]{1,0:T(8,128)(2,1)} %param.24) | copy-start | bytes 1769476
  305.7 221.5 %collective-permute-start.28 = (f32[4,384,384]{2,1,0:T(8,128)}, f32[4,384,384]{2,1,0:T(8,128)}, u32[]{:S(2)}, u32[]{:S(2)}) collective-permute-start(f32[4,384,384]{2,1,0:T(8,128)} %pad_maximum_fusion.2.near_ref), channel_id=1, source_target_pairs={{0,2},{1,5},{2,0},{3,7},{4,6},{5,1},{6,4},{7,3},{8,10},{9,13},{10,... | collective-permute-start | bytes 7077896 | tf_op jit(solution)/shard_map/ppermute | solution.py:114
  329.9 49.5 %copy-start.19 = (f32[512,768]{1,0:T(8,128)S(1)}, f32[512,768]{1,0:T(8,128)}, u32[]{:S(2)}) copy-start(f32[512,768]{1,0:T(8,128)} %copy-done.18) | copy-start | bytes 4718596
  329.9 342.2 %collective-permute-start.10 = (f32[4,384,384]{2,1,0:T(8,128)}, f32[4,384,384]{2,1,0:T(8,128)}, u32[]{:S(2)}, u32[]{:S(2)}) collective-permute-start(f32[4,384,384]{2,1,0:T(8,128)} %pad_maximum_fusion.near_ref), channel_id=1, source_target_pairs={{0,2},{1,5},{2,0},{3,7},{4,6},{5,1},{6,4},{7,3},{8,10},{9,13},{10,... | collective-permute-start | bytes 7077896 | tf_op jit(solution)/shard_map/ppermute | solution.py:114
  332.8 46.6 %collective-permute-start.3 = (f32[512,768]{1,0:T(8,128)}, f32[512,768]{1,0:T(8,128)}, u32[]{:S(2)}, u32[]{:S(2)}) collective-permute-start(f32[512,768]{1,0:T(8,128)} %add_add_fusion), channel_id=1, source_target_pairs={{0,1},{1,0},{2,3},{3,2},{4,5},{5,4},{6,7},{7,6},{8,9},{9,8},{10,11... | collective-permute-start | bytes 4718600 | tf_op jit(solution)/shard_map/ppermute | solution.py:106
  333.1 27.6 %collective-permute-start.11 = (f32[18,384]{1,0:T(8,128)S(1)}, f32[18,384]{1,0:T(8,128)S(1)}, u32[]{:S(2)}, u32[]{:S(2)}) collective-permute-start(f32[18,384]{1,0:T(8,128)S(1)} %reshape.158), channel_id=1, source_target_pairs={{0,2},{1,3},{2,0},{3,1},{4,6},{5,7},{6,4},{7,5},{8,10},{9,11},{10,... | collective-permute-start | bytes 82952 | tf_op jit(solution)/shard_map/ppermute | solution.py:114
  360.8 4.0 collective-permute-start.12
  364.8 4.0 collective-permute-start.13
  368.8 5.8 collective-permute-start.14
  527.2 289.7 %copy-start.1 = (bf16[768,1536]{1,0:T(8,128)(2,1)S(1)}, bf16[768,1536]{1,0:T(8,128)(2,1)}, u32[]{:S(2)}) copy-start(bf16[768,1536]{1,0:T(8,128)(2,1)} %param.30) | copy-start | bytes 7077892
  (38 other events, 97.5 us)

commit v2 on v0

v2 whole, which is shorter than its diff:
```python
import functools

import jax
import jax.numpy as jnp
import numpy as np
from jax import lax
from jax.experimental import pallas as pl
from jax.experimental.pallas import tpu as pltpu
from jax.sharding import PartitionSpec as P

DH = 64
BLOCK = 384
HALF = 192
CUBE = 16
MIB = 1 << 20

norm_eps = 1e-12
score_scale = 0.125
root_half = 0.7071067811865476
inv_root_two_pi = 0.3989422804014327

PLAN = {"D": "Q", "E": "P", "U": "P", "V": "P", "R": "S", "S": "P"}
ORDER = (
    ("D1", "E1", "keep", "ffn", "V1", "mid", "back", "cut", "tail", "E2", "D2", "V2", "U1", "S1", "E3", "V3"),
    ("R1", "E4", "D3", "V4", "E5", "R2", "E6", "D4", "S2", "V5", "R3", "U2", "R4", "D5", "V6", "S3"),
    ("U3", "E7", "R5", "V7", "S4", "R6", "D6", "U4", "S5", "Vj", "fin", "R7", "U5", "S6", "D7", "U6"),
    ("Ej", "S7", "Rj", "U7", "Sj", "Dj", "vec", "Uj"),
)
ROUTES = {
    "P": ((1, 2), (2, 1), (4, 4)),
    "S": ((1, 2), (4, 4), (2, 1)),
    "Q": ((4, 4), (1, 2), (2, 1)),
}
ACROSS = (12, 12)


def coordinate(rank, mask):
    if mask == 1:
        return rank & 1
    if mask == 2:
        return (rank >> 1) & 1
    return ((rank >> 2) ^ (rank >> 3)) & 1


def block_places(name):
    sub = HALF * (name in "EVS")
    places = []
    for block in range(8):
        high, low = block >> 1, block & 1
        if name in "DE":
            row, column = high * BLOCK + sub, low * BLOCK
            places.append((0, row, column, row, column))
        elif name in "UV":
            row, column = low * BLOCK + sub, high * BLOCK
            places.append((0, row, column, row, column))
        elif high < 3:
            row = low * BLOCK + sub
            places.append((high, row, 0, row, high * BLOCK))
        else:
            places.append((3, sub, low * BLOCK, 2 * BLOCK + sub, (3 + low) * BLOCK))
    return places


def device_tables(ranks):
    rows = []
    for rank in range(ranks):
        for core in range(2):
            row = []
            for name, route in PLAN.items():
                first, second, third = [coordinate(rank, pair[core]) for pair in ROUTES[route]]
                mine = 4 * first + 2 * second + third
                places = block_places(name)
                row += [places[spot ^ mine][3] for spot in range(8)]
                row += [places[spot ^ mine][4] for spot in range(8)]
                near = [(block ^ mine) & 3 for block in range(8)]
                far = list(near)
                for block in range(8):
                    edge = 4 if block < 4 else 3
                    if block >> 2 == first:
                        far[block] = near[edge]
                    else:
                        near[block] = (edge ^ mine) & 3
                row += near + far + [first]
            rows.append(row)
    return np.array(rows, np.int32)


TABLE = 33
PIECES = 4


def matmul(left, right):
    return jnp.dot(left, right, preferred_element_type=jnp.float32)


def matmul_flip(left, right):
    return lax.dot_general(
        left, right, (((1,), (1,)), ((), ())), preferred_element_type=jnp.float32
    )


def outer_sum(left, right):
    return lax.dot_general(
        left, right, (((0,), (0,)), ((), ())), preferred_element_type=jnp.float32
    )


def wide(ref):
    return ref[...].astype(jnp.float32)


def across(ref):
    return wide(ref).reshape(1, -1)


def row_mean(value):
    return jnp.mean(value, axis=-1, keepdims=True)


def norm_parts(value):
    center = value - row_mean(value)
    scale = lax.rsqrt(row_mean(center * center) + norm_eps)
    return center * scale, scale


def norm_lower(along, normal, scale):
    return scale * (along - row_mean(along) - normal * row_mean(along * normal))


def column_sum(value):
    return jnp.sum(value, axis=0, keepdims=True)


def cost(flops, bytes_accessed, transcendentals=0):
    return pl.CostEstimate(flops=1, bytes_accessed=1, transcendentals=0)


def call(kernel, ins, outs, estimate, limit, scalars=1, scratch=()):
    specs = [
        pl.BlockSpec(memory_space=pltpu.SMEM if place < scalars else pltpu.VMEM)
        for place in range(len(ins))
    ]
    return pl.pallas_call(
        kernel,
        out_shape=tuple(jax.ShapeDtypeStruct(shape, kind) for shape, kind in outs),
        in_specs=specs,
        out_specs=tuple(pl.BlockSpec(memory_space=pltpu.VMEM) for _ in outs),
        scratch_shapes=list(scratch),
        compiler_params=pltpu.CompilerParams(vmem_limit_bytes=limit * MIB),
        cost_estimate=estimate,
    )(*ins)


def head_of(lanes, head):
    return (lanes // DH) == head


def scores_flip(keys, query, limit):
    scores = matmul_flip(keys, query)
    visible = lax.broadcasted_iota(jnp.int32, scores.shape, 0) < limit
    return jnp.where(visible, scores, -1e30)


def attend_kernel(
    lengths, tokens, query_weight, query_bias, key_weight, value_weight, value_bias, out_weight,
    query_ref, keys_ref, values_ref, context_ref, log_ref, partial_ref,
):
    inputs = tokens[...]
    query_ref[...] = (matmul(inputs, query_weight[...]) + across(query_bias)).astype(jnp.bfloat16)
    keys_ref[...] = matmul(inputs, key_weight[...]).astype(jnp.bfloat16)
    values_ref[...] = (matmul(inputs, value_weight[...]) + across(value_bias)).astype(jnp.bfloat16)
    limit = lengths[0]
    for pair in range(query_ref.shape[1] // (2 * DH)):
        columns = slice(pair * 2 * DH, (pair + 1) * 2 * DH)
        query = query_ref[:, columns] * jnp.bfloat16(score_scale)
        keys = keys_ref[:, columns]
        values = values_ref[:, columns]
        lanes = lax.broadcasted_iota(jnp.int32, query.shape, 1)
        sides = []
        for head in range(2):
            scores = scores_flip(keys, jnp.where(head_of(lanes, head), query, 0), limit)
            top = jnp.max(scores, axis=0, keepdims=True)
            raised = jnp.exp(scores - top)
            total = jnp.sum(raised, axis=0, keepdims=True)
            chances = (raised * (1.0 / total)).astype(jnp.bfloat16)
            log_ref[2 * pair + head : 2 * pair + head + 1, :] = top + jnp.log(total)
            sides.append(outer_sum(values, chances))
        rows = lax.broadcasted_iota(jnp.int32, sides[0].shape, 0)
        context = jnp.where(head_of(rows, 0), sides[0], sides[1])
        context_ref[:, columns] = context.T.astype(jnp.bfloat16)
    partial_ref[...] = matmul(context_ref[...], out_weight[...])


def attend(lengths, tokens, query_weight, query_bias, key_weight, value_weight, value_bias, out_weight):
    rows, width = tokens.shape
    columns = query_weight.shape[1]
    narrow = ((rows, columns), jnp.bfloat16)
    return call(
        attend_kernel,
        (lengths, tokens, query_weight, query_bias, key_weight, value_weight, value_bias, out_weight),
        (narrow, narrow, narrow, narrow, ((8, rows), jnp.float32), ((rows, width), jnp.float32)),
        cost(8 * rows * width * columns + 8 * rows * rows * columns, 8 * MIB),
        limit=56,
    )


def phi(before):
    return 0.5 * (1.0 + lax.erf(before * root_half))


def ffn_kernel(
    tokens, own, got, out_bias, mid_gain, mid_shift, up_weight, up_bias, down_weight,
    normal_ref, scale_ref, low_ref, before_ref, active_ref, partial_ref,
):
    normal, scale = norm_parts(wide(tokens) + (own[...] + got[...]) + across(out_bias))
    normal_ref[...] = normal
    scale_ref[...] = scale
    low_ref[...] = (normal * across(mid_gain) + across(mid_shift)).astype(jnp.bfloat16)
    hidden = up_weight.shape[1]
    bias = across(up_bias)
    for start in range(0, hidden, 256):
        columns = slice(start, start + 256)
        before = matmul(low_ref[...], up_weight[:, columns]) + bias[:, columns]
        before_ref[:, columns] = before
        active_ref[:, columns] = (before * phi(before)).astype(jnp.bfloat16)
    partial_ref[...] = matmul(active_ref[...], down_weight[...])


def ffn(tokens, own, got, out_bias, mid_gain, mid_shift, up_weight, up_bias, down_weight):
    rows, width = tokens.shape
    hidden = up_weight.shape[1]
    full = ((rows, width), jnp.float32)
    return call(
        ffn_kernel,
        (tokens, own, got, out_bias, mid_gain, mid_shift, up_weight, up_bias, down_weight),
        (
            full,
            ((rows, 1), jnp.float32),
            ((rows, width), jnp.bfloat16),
            ((rows, hidden), jnp.float32),
            ((rows, hidden), jnp.bfloat16),
            full,
        ),
        cost(4 * rows * width * hidden, 16 * MIB, rows * hidden),
        scalars=0,
        limit=56,
    )


def cut(offsets, flipped, right, targets, first, spots):
    for part in range(2):
        base = (first + part) * TABLE
        for place, spot in enumerate(spots):
            row = pl.multiple_of(offsets[base + spot], HALF // 12)
            column = pl.multiple_of(offsets[base + 8 + spot], 128)
            targets[part][place * HALF : (place + 1) * HALF, :] = matmul(
                flipped[pl.ds(row, HALF), :], right[:, pl.ds(column, BLOCK)]
            )


KEPT = (0, 1, 2, 3)
SENT = (4, 5, 6, 7)


def flip_into(flipped, left, start=0):
    for column in range(0, left.shape[1], 128):
        flipped[start + column : start + column + 128, :] = left[:, column : column + 128].T


SUMS = 16
blocks = ((4 * HALF, BLOCK), jnp.float32)
blocks_and_sums = ((4 * HALF + 2 * SUMS, BLOCK), jnp.float32)


def sums(width):
    return ((8, width), jnp.float32)


def flip_kernel(value, flipped_ref):
    for column in range(0, value.shape[1], 128):
        flipped_ref[column : column + 128, :] = value[:, column : column + 128].T


def flip(value):
    return call(
        flip_kernel, (value,), ((value.shape[::-1], value.dtype),), cost(0, 4 * value.size), scalars=0, limit=56
    )[0]


def last_kernel(
    offsets, normal, mid_gain, mid_shift, own, got, down_bias, final_gain, cotangent, flipped,
    second_ref, low_ref, final_ref, send0, send1,
):
    middle = normal[...] * across(mid_gain) + across(mid_shift)
    final, scale = norm_parts(middle + (own[...] + got[...]) + across(down_bias))
    final_ref[...] = final
    second = norm_lower(wide(cotangent) * across(final_gain), final, scale)
    low_ref[...] = second.astype(jnp.bfloat16)
    second_ref[...] = second
    cut(offsets, flipped, low_ref, (send0, send1), 0, SENT)


def last(offsets, normal, mid_gain, mid_shift, own, got, down_bias, final_gain, cotangent, flipped):
    rows, width = normal.shape
    full = ((rows, width), jnp.float32)
    return call(
        last_kernel,
        (offsets, normal, mid_gain, mid_shift, own, got, down_bias, final_gain, cotangent, flipped),
        (full, ((rows, width), jnp.bfloat16), full, blocks, blocks),
        cost(rows * width * flipped.shape[0], 14 * MIB),
        limit=56,
    )


def keep_kernel(
    offsets, second, low, final, final_gain, final_shift, cotangent, flipped, out_ref, sums_ref, keep0, keep1
):
    cut(offsets, flipped, low, (keep0, keep1), 0, KEPT)
    upper = wide(cotangent)
    sums_ref[...] = jnp.zeros_like(sums_ref)
    sums_ref[0:1, :] = column_sum(second[...])
    sums_ref[1:2, :] = column_sum(upper * final[...])
    sums_ref[2:3, :] = column_sum(upper)
    out_ref[...] = (final[...] * across(final_gain) + across(final_shift)).astype(jnp.bfloat16)


def keep(offsets, second, low, final, final_gain, final_shift, cotangent, flipped):
    rows, width = low.shape
    return call(
        keep_kernel,
        (offsets, second, low, final, final_gain, final_shift, cotangent, flipped),
        (((rows, width), jnp.bfloat16), sums(width), blocks, blocks),
        cost(rows * width * flipped.shape[0], 14 * MIB),
        limit=26,
    )


def ffn_back_kernel(
    offsets, second_low, down_weight, before_ref, low, up_weight,
    sums_ref, send0, keep0, send1, keep1, *rest,
):
    partial_refs, before_grad, flipped = rest[:PIECES], rest[-2], rest[-1]
    hidden = before_ref.shape[1]
    width = sums_ref.shape[1]
    sums_ref[...] = jnp.zeros_like(sums_ref)
    for start in range(0, hidden, 256):
        columns = slice(start, start + 256)
        before = before_ref[:, columns]
        slope = phi(before) + before * inv_root_two_pi * jnp.exp(-0.5 * before * before)
        grad = (matmul_flip(second_low[...], down_weight[columns, :]) * slope).astype(jnp.bfloat16)
        before_grad[:, columns] = grad
        row, place = start // width, start % width
        sums_ref[row : row + 1, place : place + 256] = column_sum(grad.astype(jnp.float32))
    for place, partial_ref in enumerate(partial_refs):
        rows = slice(place * partial_ref.shape[0], (place + 1) * partial_ref.shape[0])
        partial_ref[...] = matmul_flip(before_grad[rows, :], up_weight[...])
    flip_into(flipped, low)
    cut(offsets, flipped, before_grad, (send0, send1), 2, SENT)
    cut(offsets, flipped, before_grad, (keep0, keep1), 2, KEPT)


def ffn_back(offsets, second_low, down_weight, before, low, up_weight):
    rows, width = low.shape
    hidden = before.shape[1]
    return call(
        ffn_back_kernel,
        (offsets, second_low, down_weight, before, low, up_weight),
        (sums(width), blocks, blocks, blocks, blocks) + (((rows // PIECES, width), jnp.float32),) * PIECES,
        cost(6 * rows * width * hidden, 18 * MIB, 2 * rows * hidden),
        scratch=[pltpu.VMEM((rows, hidden), jnp.bfloat16), pltpu.VMEM((width, rows), jnp.bfloat16)],
        limit=26,
    )


def mid_kernel(second, normal_ref, scale, mid_gain, out_weight, *rest):
    own, got = rest[:PIECES], rest[PIECES : 2 * PIECES]
    first_ref, low_ref, context_grad, sums_ref, upper = rest[2 * PIECES :]
    for place in range(PIECES):
        rows = slice(place * own[place].shape[0], (place + 1) * own[place].shape[0])
        upper[rows, :] = second[rows, :] + (own[place][...] + got[place][...])
    normal = normal_ref[...]
    sums_ref[...] = jnp.zeros_like(sums_ref)
    sums_ref[1:2, :] = column_sum(upper[...] * normal)
    sums_ref[2:3, :] = column_sum(upper[...])
    first = norm_lower(upper[...] * across(mid_gain), normal, scale[...])
    sums_ref[0:1, :] = column_sum(first)
    first_ref[...] = first
    low_ref[...] = first.astype(jnp.bfloat16)
    context_grad[...] = matmul_flip(low_ref[...], out_weight[...]).astype(jnp.bfloat16)


def mid(second, own, got, normal, scale, mid_gain, out_weight):
    rows, width = second.shape
    columns = out_weight.shape[0]
    return call(
        mid_kernel,
        (second, normal, scale, mid_gain, out_weight, *own, *got),
        (
            ((rows, width), jnp.float32),
            ((rows, width), jnp.bfloat16),
            ((rows, columns), jnp.bfloat16),
            sums(width),
        ),
        cost(2 * rows * width * columns, 10 * MIB),
        scalars=0,
        scratch=[pltpu.VMEM((rows, width), jnp.float32)],
        limit=20,
    )


def attend_back_kernel(
    lengths, query_ref, keys_ref, values_ref, log_ref, upstream_ref,
    grads_ref, sums_ref,
):
    limit = lengths[0]
    sums_ref[...] = jnp.zeros_like(sums_ref)
    width = query_ref.shape[1]
    for pair in range(width // (2 * DH)):
        columns = slice(pair * 2 * DH, (pair + 1) * 2 * DH)
        query = query_ref[:, columns] * jnp.bfloat16(score_scale)
        keys = keys_ref[:, columns]
        values = values_ref[:, columns]
        upstream = upstream_ref[:, columns]
        lanes = lax.broadcasted_iota(jnp.int32, query.shape, 1)
        value_grad = jnp.zeros(query.shape, jnp.float32)
        key_grad = jnp.zeros(query.shape, jnp.float32)
        sides = []
        for head in range(2):
            mine = head_of(lanes, head)
            asked = jnp.where(mine, query, 0)
            pulled = jnp.where(mine, upstream, 0)
            scores = scores_flip(keys, asked, limit)
            chances = jnp.exp(scores - log_ref[2 * pair + head : 2 * pair + head + 1, :])
            value_grad = value_grad + matmul(chances.astype(jnp.bfloat16), pulled)
            spread = matmul_flip(values, pulled).astype(jnp.bfloat16).astype(jnp.float32)
            common = jnp.sum(spread * chances, axis=0, keepdims=True)
            score_grad = (chances * (spread - common)).astype(jnp.bfloat16)
            key_grad = key_grad + matmul(score_grad, asked)
            sides.append(outer_sum(keys, score_grad))
        rows = lax.broadcasted_iota(jnp.int32, sides[0].shape, 0)
        query_grad = (jnp.where(head_of(rows, 0), sides[0], sides[1]).T * score_scale).astype(jnp.bfloat16)
        key_low = key_grad.astype(jnp.bfloat16)
        value_low = value_grad.astype(jnp.bfloat16)
        grads_ref[:, columns] = query_grad
        grads_ref[:, slice(width + columns.start, width + columns.stop)] = key_low
        grads_ref[:, slice(2 * width + columns.start, 2 * width + columns.stop)] = value_low
        sums_ref[0:1, columns] = column_sum(query_grad.astype(jnp.float32))
        sums_ref[0:1, slice(width + columns.start, width + columns.stop)] = column_sum(
            value_low.astype(jnp.float32)
        )


def attend_back(lengths, query, keys, values, log_total, upstream):
    rows, width = query.shape
    return call(
        attend_back_kernel,
        (lengths, query, keys, values, log_total, upstream),
        (((rows, 3 * width), jnp.bfloat16), sums(2 * width)),
        cost(20 * rows * rows * width, 4 * MIB, rows * rows * width // DH),
        limit=16,
    )


def rest_kernel(
    offsets, tokens, context, grads, first_low, last_sums, up_sums, mid_sums, back_sums,
    send0, keep0, send1, keep1, flipped, right,
):
    flip_into(flipped, tokens)
    flip_into(flipped, context, tokens.shape[1])
    right[:, : grads.shape[1]] = grads[...]
    right[:, grads.shape[1] :] = first_low[...]
    cut(offsets, flipped, right, (send0, send1), 4, SENT)
    cut(offsets, flipped, right, (keep0, keep1), 4, KEPT)
    rows = [last_sums[0:3, :], up_sums[0:2, :], mid_sums[0:3, :], back_sums[0:1, :]]
    send1[4 * HALF :, :] = jnp.zeros((2 * SUMS, BLOCK), jnp.float32)
    for half in range(2):
        place = 4 * HALF + half * SUMS
        for part in rows:
            send1[place : place + part.shape[0], :] = part[:, half * BLOCK : (half + 1) * BLOCK]
            place = place + part.shape[0]


def rest(offsets, tokens, context, grads, first_low, last_sums, up_sums, mid_sums, back_sums):
    rows, width = tokens.shape
    left = width + context.shape[1]
    right = grads.shape[1] + width
    return call(
        rest_kernel,
        (offsets, tokens, context, grads, first_low, last_sums, up_sums, mid_sums, back_sums),
        (blocks, blocks, blocks_and_sums, blocks),
        cost(32 * rows * HALF * BLOCK, 8 * MIB),
        scratch=[pltpu.VMEM((left, rows), jnp.bfloat16), pltpu.VMEM((rows, right), jnp.bfloat16)],
        limit=16,
    )


def input_kernel(grads, query_weight, key_weight, value_weight, partial_ref):
    width = query_weight.shape[1]
    partial_ref[...] = (
        matmul_flip(grads[:, :width], query_weight[...])
        + matmul_flip(grads[:, width : 2 * width], key_weight[...])
        + matmul_flip(grads[:, 2 * width :], value_weight[...])
    )


def input_part(grads, query_weight, key_weight, value_weight):
    rows, width = grads.shape[0], query_weight.shape[0]
    return call(
        input_kernel,
        (grads, query_weight, key_weight, value_weight),
        (((rows, width), jnp.float32),),
        cost(2 * rows * width * grads.shape[1], 6 * MIB),
        scalars=0,
        limit=10,
    )[0]


def join_kernel(name, table, near, far, *rest):
    places = block_places(name)
    count = len({place[0] for place in places})
    outs, done = rest[-count - 1 : -1], rest[-1]
    for side in range(2):

        @pl.when(table[16] == side)
        def _():
            copies = []
            for block in range(8):
                out, row, column = places[block][:3]
                source = near if block >> 2 == side else far
                copies.append(
                    pltpu.make_async_copy(
                        source.at[pl.ds(pl.multiple_of(table[8 * (source is far) + block] * HALF, 8), HALF)],
                        outs[out].at[pl.ds(row, HALF), pl.ds(column, BLOCK)],
                        done.at[block],
                    )
                )
            for copy in copies:
                copy.start()
            for copy in copies:
                copy.wait()


def join(name, table, near, far, shapes, earlier):
    specs = [
        pl.BlockSpec(memory_space=pltpu.SMEM),
        pl.BlockSpec(memory_space=pltpu.VMEM),
        pl.BlockSpec(memory_space=pltpu.VMEM),
    ] + [pl.BlockSpec(memory_space=pl.ANY) for _ in earlier]
    return pl.pallas_call(
        functools.partial(join_kernel, name),
        out_shape=tuple(jax.ShapeDtypeStruct(shape, jnp.float32) for shape in shapes),
        in_specs=specs,
        out_specs=tuple(pl.BlockSpec(memory_space=pl.ANY) for _ in shapes),
        scratch_shapes=[pltpu.SemaphoreType.DMA((8,))],
        input_output_aliases={3 + place: place for place in range(len(earlier))},
        compiler_params=pltpu.CompilerParams(vmem_limit_bytes=16 * MIB),
        cost_estimate=cost(0, 64 * HALF * BLOCK),
    )(table, near, far, *earlier)


def swap_cores(part):
    return lax.ppermute(part, "mp", [(0, 1), (1, 0)])


def hop(block, masks, ranks):
    pairs = [
        (2 * rank + core, 2 * (rank ^ masks[core]) + core) for rank in range(ranks) for core in (0, 1)
    ]
    return lax.ppermute(block, ("dp", "mp"), pairs)


def tied(value, before):
    return value if before is None else lax.optimization_barrier((value, before))[0]


class Sum:
    def __init__(self, name, send, keep, ranks):
        self.name, self.send, self.keep, self.ranks = name, send, keep, ranks
        self.masks = ROUTES[PLAN[name]] + (ACROSS,)
        self.got = {}
        self.extra = send[4 * HALF :] if send.shape[0] > 4 * HALF else None

    def with_extra(self, value, got, rows):
        if self.extra is None:
            return value
        self.extra = self.extra + got[rows:]
        return jnp.concatenate([value, self.extra])

    def step(self, number, before):
        got, one, two = self.got, HALF, 2 * HALF
        keep = tied(self.own if number > 4 else self.keep if number > 1 else self.send, before)
        if number == 1:
            value = keep
        elif number == 2:
            value = self.with_extra(keep[two:] + got[1][two : 2 * two], got[1], 2 * two)
        elif number == 3:
            value = self.with_extra(keep[one:two] + got[1][one:two] + got[2][one:two], got[2], two)
        elif number == 4:
            value = keep[:one] + got[1][:one] + got[2][:one] + got[3][:one]
            value = self.with_extra(value, got[3], one)
        elif number == 5:
            value = keep + got[4]
            bit = CUBE
            while bit < self.ranks:
                value = value + hop(value, (bit, bit), self.ranks)
                bit = 2 * bit
            if self.extra is not None:
                value, self.extra = value[:one], value[one:]
        elif number == 6:
            value = jnp.concatenate([keep, got[5]])
        else:
            value = jnp.concatenate([keep, got[6]])
        self.own = value
        with jax.named_scope(f"{self.name}{number}"):
            got[number] = hop(value, self.masks[min(number, 8 - number) - 1], self.ranks)
        return value


def body(
    ranks,
    tables,
    tokens,
    lengths,
    cotangent,
    query_weight,
    query_bias,
    key_weight,
    value_weight,
    value_bias,
    out_weight,
    out_bias,
    mid_gain,
    mid_shift,
    up_weight,
    up_bias,
    down_weight,
    down_bias,
    final_gain,
    final_shift,
):
    table = jnp.asarray(tables)[2 * lax.axis_index("dp") + lax.axis_index("mp")]
    width = tokens.shape[1]
    columns = query_weight.shape[1]
    hidden = up_weight.shape[1]

    query, keys, values, context, log_total, partial = attend(
        lengths, tokens, query_weight, query_bias, key_weight, value_weight, value_bias, out_weight
    )
    mid_normal, mid_scale, mid_low, before, active, down_partial = ffn(
        tokens, partial, swap_cores(partial), out_bias, mid_gain, mid_shift,
        up_weight, up_bias, down_weight,
    )
    active_flip = flip(active)
    second_grad, second_low, final_normal, *down_sent = last(
        table, mid_normal, mid_gain, mid_shift, down_partial, swap_cores(down_partial),
        down_bias, final_gain, cotangent, active_flip,
    )
    parts = {
        "D": Sum("D", down_sent[0], None, ranks),
        "E": Sum("E", down_sent[1], None, ranks),
    }
    point = None
    joined = {}
    for item in sum(ORDER, ()):
        if item == "keep":
            layer_out, last_sums, *down_kept = keep(
                table, second_grad, tied(second_low, point), final_normal, final_gain, final_shift,
                cotangent, active_flip,
            )
            parts["D"].keep, parts["E"].keep = down_kept
            point = down_kept[0]
        elif item == "ffn":
            up_sums, *up_cut = ffn_back(
                table, tied(second_low, point), down_weight, before, mid_low, up_weight
            )
            parts["U"] = Sum("U", up_cut[0], up_cut[1], ranks)
            parts["V"] = Sum("V", up_cut[2], up_cut[3], ranks)
            up_partial = up_cut[4:]
            up_got = [swap_cores(piece) for piece in up_partial]
            point = up_cut[0]
        elif item == "mid":
            first_grad, first_low, context_grad, mid_sums = mid(
                tied(second_grad, point), up_partial, up_got, mid_normal, mid_scale, mid_gain, out_weight
            )
            point = context_grad
        elif item == "back":
            grads, back_sums = attend_back(
                lengths, query, keys, values, log_total, tied(context_grad, point)
            )
            point = grads
        elif item == "cut":
            rest_cut = rest(
                table, tokens, context, tied(grads, point), first_low, last_sums, up_sums, mid_sums, back_sums
            )
            parts["R"] = Sum("R", rest_cut[0], rest_cut[1], ranks)
            parts["S"] = Sum("S", rest_cut[2], rest_cut[3], ranks)
            point = rest_cut[0]
        elif item == "tail":
            partial = input_part(tied(grads, point), query_weight, key_weight, value_weight)
            partial_got = swap_cores(partial)
            point = partial
        elif item == "fin":
            input_grad = (first_grad + (tied(partial, point) + partial_got)).astype(jnp.bfloat16)
            point = input_grad
        elif item == "vec":
            small = tied(parts["S"].extra, point).reshape(2, SUMS, BLOCK)
            small = jnp.concatenate([small[0], small[1]], axis=1)
            down_bias_grad, final_gain_grad, final_shift_grad = small[0], small[1], small[2]
            up_bias_grad = small[3 : 3 + hidden // width].reshape(-1)
            out_bias_grad, mid_gain_grad, mid_shift_grad = small[5], small[6], small[7]
            query_bias_grad, value_bias_grad = small[8, :columns], small[8, columns : 2 * columns]
            point = value_bias_grad
        elif item[1] == "j":
            family = {"E": "D", "V": "U", "S": "R"}.get(item[0], item[0])
            shapes = {
                "D": [(hidden, width)],
                "U": [(width, hidden)],
                "R": [(width, columns)] * 3 + [(columns, width)],
            }[family]
            place = list(PLAN).index(item[0]) * TABLE + 16
            part = parts[item[0]]
            joined[family] = join(
                item[0], table[place : place + 17], tied(part.own, point), part.got[7], shapes,
                joined.get(family, ()),
            )
            point = joined[family][0]
        else:
            point = parts[item[0]].step(int(item[1]), point)
    (down_weight_grad,), (up_weight_grad,) = joined["D"], joined["U"]
    query_weight_grad, key_weight_grad, value_weight_grad, out_weight_grad = joined["R"]
    return (
        layer_out,
        input_grad,
        query_weight_grad,
        query_bias_grad,
        key_weight_grad,
        value_weight_grad,
        value_bias_grad,
        out_weight_grad,
        out_bias_grad,
        mid_gain_grad,
        mid_shift_grad,
        up_weight_grad,
        up_bias_grad,
        down_weight_grad,
        down_bias_grad,
        final_gain_grad,
        final_shift_grad,
    )


def solution(mesh):
    rows, whole, split, vector = P("dp", None), P(), P(None, "mp"), P("mp")
    across = P("mp", None)
    in_specs = (
        rows, P("dp"), rows, split, vector, split, split, vector, across, whole, whole, whole,
        split, vector, across, whole, whole, whole,
    )
    out_specs = (
        rows, rows, split, vector, split, split, vector, across, whole, whole, whole,
        split, vector, across, whole, whole, whole,
    )
    ranks = mesh.shape["dp"]
    return jax.shard_map(
        functools.partial(body, ranks, device_tables(ranks)),
        mesh=mesh, in_specs=in_specs, out_specs=out_specs, check_vma=False,
    )
```

time: 682 us -> 262 us (0.38)
  waiting for transfers between devices: 436 us -> 110 us
  local copies, waits for them, and re-layouts: 148 us -> 11.2 us
  Pallas kernels: 0 us -> 62 us
  starting transfers between devices: 0.61 us -> 60.4 us
  matrix products: 51.4 us -> 0 us
  between operations: 15 us -> 2.31 us
  other arithmetic: 24.9 us -> 15.1 us
    psum x5 -> x0, waiting for transfers between devices: 436 us -> none  [the longest x1 395 us: body(): summed = unflatten(lax.psum(flatten(every), 'dp'), every)]
    ppermute x0 -> x49, waiting for transfers between devices: none -> 110 us  [the longest x42 105 us: hop(): return lax.ppermute(block, ('dp', 'mp'), pairs)]
    unnamed x132 -> x86, local copies, waits for them, and re-layouts: 95.6 us -> 7.38 us
    pallas_call x0 -> x16, Pallas kernels: none -> 62 us  [the longest x10 50 us: call(): pl.pallas_call(kernel, out_shape=tuple((jax.ShapeDtypeStruct(shape, kind)...]
    ppermute x0 -> x49, starting transfers between devices: none -> 60.4 us  [the longest x42 58.8 us: hop(): return lax.ppermute(block, ('dp', 'mp'), pairs)]
    dot_general x24 -> x0, matrix products: 51.4 us -> none  [the longest x6 17.5 us: matmul(): return jnp.dot(left, right, preferred_element_type=jnp.float32)]
    slice x10 -> x5, local copies, waits for them, and re-layouts: 26.4 us -> 1.58 us  [the longest x1 0.95 us: body(): table[place:place + 17]]
    reshape x7 -> x1, local copies, waits for them, and re-layouts: 21.8 us -> 0.61 us  [body(): up_bias_grad = small[3:3 + hidden // width].reshape(-1)]
  transfers between devices with their start and end apart: 5 -> 49, of which waited for: 3 -> 27; matrix products, arithmetic and copies ran while one was open for 19% -> 7% of each run, Pallas kernels for 0% -> 14%
where the time goes in v2:
time: 262 us; the launch traced here: 261 us
  waiting for transfers between devices  110 us (42%)
  Pallas kernels  62 us (24%)
  starting transfers between devices  60.4 us (23%)
  other arithmetic  15.1 us (6%)
  local copies, waits for them, and re-layouts  11.2 us (4%)
    ppermute x42, waiting for transfers between devices, hop(): return lax.ppermute(block, ('dp', 'mp'), pairs)  105 us
    ppermute x42, starting transfers between devices, hop(): return lax.ppermute(block, ('dp', 'mp'), pairs)  58.8 us
    pallas_call x10, Pallas kernels, call(): pl.pallas_call(kernel, out_shape=tuple((jax.ShapeDtypeStruct(shape, kind)...  50 us
    pallas_call x6, Pallas kernels, join(): pl.pallas_call(functools.partial(join_kernel, name), out_shape=tuple((jax...  12.1 us
    unnamed x86, local copies, waits for them, and re-layouts  7.38 us
    ppermute x7, waiting for transfers between devices, swap_cores(): return lax.ppermute(part, 'mp', [(0, 1), (1, 0)])  5.66 us
  transfers between devices with their start and end apart: 49, of which 27 were waited for; matrix products, arithmetic and copies ran while one was open for 7% of the time, Pallas kernels for 14%

profile of v2, /device:TPU:0, one launch (start us, length us, event | category | flops | bytes accessed | tf_op | source)
XLA Modules:
  0.0 261.4 jit_solution(1202487632268535938)
XLA Ops:
  1.3 8.2 %shard_map.314 = (bf16[512,384]{1,0:T(8,128)(2,1)}, bf16[512,384]{1,0:T(8,128)(2,1)}, bf16[512,384]{1,0:T(8,128)(2,1)}, bf16[512,384]{1,0:T(8,128)(2,1)}, f32[8,512]{1,0:T(8,128)}, /*index=5*/f32[512,768]{1,0:T(8,128)}) custom-call(s32[1]{0:T(128)S(6)} %copy.60.lengths, bf16[512,768]{1,0:T(8,128)(2,1)} %tokens.5, bf16[768,384]{1,0:T(8,128)(2,1)} %query_weight.3, ...), custom_call_target="tpu_custom_call" | custom-call | flops 1 | bytes 1 | tf_op jit(solution)/shard_map/pallas_call | solution.py:143
  9.9 3.2 %collective-permute-done.got = f32[512,768]{1,0:T(8,128)S(1)} collective-permute-done((f32[512,768]{1,0:T(8,128)}, f32[512,768]{1,0:T(8,128)S(1)}, u32[]{:S(2)}, u32[]{:S(2)}) %collective-permute-start) | collective-permute-done | bytes 1572896 | tf_op jit(solution)/shard_map/ppermute | solution.py:562
  14.3 8.6 %shard_map.315 = (f32[512,768]{1,0:T(8,128)}, f32[512,1]{1,0:T(8,128)}, bf16[512,768]{1,0:T(8,128)(2,1)}, f32[512,1536]{1,0:T(8,128)}, bf16[512,1536]{1,0:T(8,128)(2,1)}, /*index=5*/f32[512,768]{1,0:T(8,128)}) custom-call(bf16[512,768]{1,0:T(8,128)(2,1)} %tokens.5, f32[512,768]{1,0:T(8,128)} %get-tuple-element.119.own, f32[512,768]{1,0:T(8,128)} %copy-done.32, ...), custom_call_target="tpu_custom_call" | custom-call | flops 1 | bytes 1 | tf_op jit(solution)/shard_map/pallas_call | solution.py:143
  24.6 3.0 %shard_map.316.flipped = bf16[1536,512]{1,0:T(8,128)(2,1)} custom-call(bf16[512,1536]{1,0:T(8,128)(2,1)} %get-tuple-element.122.value), custom_call_target="tpu_custom_call" | custom-call | flops 1 | bytes 1 | tf_op jit(solution)/shard_map/pallas_call | solution.py:143
  28.8 7.6 %shard_map.317 = (f32[512,768]{1,0:T(8,128)}, bf16[512,768]{1,0:T(8,128)(2,1)}, f32[512,768]{1,0:T(8,128)}, f32[768,384]{1,0:T(8,128)}, f32[768,384]{1,0:T(8,128)}) custom-call(s32[198]{0:T(256)} %bitcast.13, f32[512,768]{1,0:T(8,128)} %get-tuple-element.120.normal.normal_ref, bf16[768]{0:T(1024)(128)(2,1)} %mid_gain.5, bf16[768]{0:T(1024)(128)(2,1)} %mid_shift.3, ...), custom_call_target="tpu_custom_call" | custom-call | flops 1 | bytes 1 | tf_op jit(solution)/shard_map/pallas_call | solution.py:143
  36.5 2.6 %collective-permute-start.6 = (f32[768,384]{1,0:T(8,128)}, f32[768,384]{1,0:T(8,128)S(1)}, u32[]{:S(2)}, u32[]{:S(2)}) collective-permute-start(f32[768,384]{1,0:T(8,128)} %get-tuple-element.127), channel_id=1, source_target_pairs={{0,2},{1,5},{2,0},{3,7},{4,6},{5,1},{6,4},{7,3},{8,10},{9,13},{10,... | collective-permute-start | bytes 3538952 | tf_op jit(solution)/shard_map/E1/ppermute | solution.py:569
  44.7 3.2 %shard_map.318 = (bf16[512,768]{1,0:T(8,128)(2,1)}, f32[8,768]{1,0:T(8,128)S(1)}, f32[768,384]{1,0:T(8,128)S(1)}, f32[768,384]{1,0:T(8,128)S(1)}) custom-call(s32[198]{0:T(256)S(1)} %bitcast.14, f32[512,768]{1,0:T(8,128)S(1)} %copy-done.5, bf16[512,768]{1,0:T(8,128)(2,1)S(1)} %copy-done.9, f32[512,768]{1,0:T(8,128)S(1)} %copy-done.14, ...), custom_call_target="tpu_custom_call" | custom-call | flops 1 | bytes 1 | tf_op jit(solution)/shard_map/pallas_call | solution.py:143
  47.9 8.3 %shard_map.319 = (f32[8,768]{1,0:T(8,128)S(1)}, f32[768,384]{1,0:T(8,128)}, f32[768,384]{1,0:T(8,128)S(1)}, f32[768,384]{1,0:T(8,128)S(1)}, f32[768,384]{1,0:T(8...) custom-call(s32[198]{0:T(256)S(1)} %bitcast.15, ...), custom_call_target="tpu_custom_call" | custom-call | flops 1 | bytes 1 | tf_op jit(solution)/shard_map/pallas_call | solution.py:143
  62.0 5.0 %shard_map.321 = (bf16[512,1152]{1,0:T(8,128)(2,1)S(1)}, f32[8,768]{1,0:T(8,128)S(1)}) custom-call(s32[1]{0:T(128)S(6)} %copy.60.lengths, bf16[512,384]{1,0:T(8,128)(2,1)S(1)} %copy-done.22, bf16[512,384]{1,0:T(8,128)(2,1)S(1)} %copy-done.23, bf16[512,384]{1,0:T(8,128)(2,1)S(1)} %copy-done.24, f32[8,512]{1,0:T(8,128)S(1)} %copy-done.28, ...), custom_call_target="tpu_custom_call" | custom-call | flops 1 | bytes 1 | tf_op jit(solution)/shard_map/pallas_call | solution.py:143
  67.1 3.0 %shard_map.322 = (f32[768,384]{1,0:T(8,128)S(1)}, f32[768,384]{1,0:T(8,128)S(1)}, f32[800,384]{1,0:T(8,128)S(1)}, f32[768,384]{1,0:T(8,128)S(1)}) custom-call(s32[198]{0:T(256)S(1)} %bitcast.16, bf16[512,768]{1,0:T(8,128)(2,1)S(1)} %copy-done.3, bf16[512,384]{1,0:T(8,128)(2,1)S(1)} %copy-done.21, bf16[512,1152]{1,0:T(8,128)(2,1)S(1)} %get-tuple-element.159.grads, ...), custom_call_target="tpu_custom_call" | custom-call | flops 1 | bytes 1 | tf_op jit(solution)/shard_map/pallas_call | solution.py:143
  76.6 10.4 %collective-permute-done.9 = f32[384,384]{1,0:T(8,128)S(1)} collective-permute-done((f32[384,384]{1,0:T(8,128)S(1)}, f32[384,384]{1,0:T(8,128)S(1)}, u32[]{:S(2)}, u32[]{:S(2)}) %collective-permute-start.9) | collective-permute-done | bytes 589856 | tf_op jit(solution)/shard_map/E2/ppermute | solution.py:569
  87.6 12.1 %collective-permute-done.10 = f32[384,384]{1,0:T(8,128)S(1)} collective-permute-done((f32[384,384]{1,0:T(8,128)S(1)}, f32[384,384]{1,0:T(8,128)S(1)}, u32[]{:S(2)}, u32[]{:S(2)}) %collective-permute-start.10) | collective-permute-done | bytes 589856 | tf_op jit(solution)/shard_map/V2/ppermute | solution.py:569
  102.4 3.7 %collective-permute-start.14 = (f32[192,384]{1,0:T(8,128)S(1)}, f32[192,384]{1,0:T(8,128)S(1)}, u32[]{:S(2)}, u32[]{:S(2)}) collective-permute-start(f32[192,384]{1,0:T(8,128)S(1)} %fusion.4), channel_id=1, source_target_pairs={{0,24},{1,25},{2,26},{3,27},{4,28},{5,29},{6,30},{7,31},{8,16},{9,... | collective-permute-start | bytes 884744 | tf_op jit(solution)/shard_map/E4/ppermute | solution.py:569
  106.1 5.6 %collective-permute-done.13 = f32[192,384]{1,0:T(8,128)S(1)} collective-permute-done((f32[192,384]{1,0:T(8,128)S(1)}, f32[192,384]{1,0:T(8,128)S(1)}, u32[]{:S(2)}, u32[]{:S(2)}) %collective-permute-start.13) | collective-permute-done | bytes 294944 | tf_op jit(solution)/shard_map/V3/ppermute | solution.py:569
  114.0 1.8 collective-permute-done.14
  116.1 5.0 %collective-permute-start.16 = (f32[192,384]{1,0:T(8,128)S(1)}, f32[192,384]{1,0:T(8,128)S(1)}, u32[]{:S(2)}, u32[]{:S(2)}) collective-permute-start(f32[192,384]{1,0:T(8,128)S(1)} %add.164), channel_id=1, source_target_pairs={{0,8},{1,9},{2,10},{3,11},{4,12},{5,13},{6,14},{7,15},{8,0},{9,1},... | collective-permute-start | bytes 884744 | tf_op jit(solution)/shard_map/E5/ppermute | solution.py:569
  123.7 5.3 %collective-permute-done.16 = f32[192,384]{1,0:T(8,128)S(1)} collective-permute-done((f32[192,384]{1,0:T(8,128)S(1)}, f32[192,384]{1,0:T(8,128)S(1)}, u32[]{:S(2)}, u32[]{:S(2)}) %collective-permute-start.16) | collective-permute-done | bytes 294944 | tf_op jit(solution)/shard_map/E5/ppermute | solution.py:569
  130.8 1.8 collective-permute-start.25
  134.7 6.1 %collective-permute-done.20 = f32[384,384]{1,0:T(8,128)} collective-permute-done((f32[384,384]{1,0:T(8,128)}, f32[384,384]{1,0:T(8,128)}, u32[]{:S(2)}, u32[]{:S(2)}) %collective-permute-start.20) | collective-permute-done | bytes 589856 | tf_op jit(solution)/shard_map/R2/ppermute | solution.py:569
  142.1 1.9 collective-permute-start.22
  146.2 2.6 %collective-permute-done.22 = f32[192,384]{1,0:T(8,128)S(1)} collective-permute-done((f32[192,384]{1,0:T(8,128)S(1)}, f32[192,384]{1,0:T(8,128)S(1)}, u32[]{:S(2)}, u32[]{:S(2)}) %collective-permute-start.22) | collective-permute-done | bytes 294944 | tf_op jit(solution)/shard_map/R3/ppermute | solution.py:569
  148.9 1.8 collective-permute-start.26
  151.9 2.7 %collective-permute-start.28 = (f32[192,384]{1,0:T(8,128)S(1)}, f32[192,384]{1,0:T(8,128)S(1)}, u32[]{:S(2)}, u32[]{:S(2)}) collective-permute-start(f32[192,384]{1,0:T(8,128)S(1)} %fusion.1), channel_id=1, source_target_pairs={{0,24},{1,25},{2,26},{3,27},{4,28},{5,29},{6,30},{7,31},{8,16},{9,... | collective-permute-start | bytes 884744 | tf_op jit(solution)/shard_map/R4/ppermute | solution.py:569
  157.1 4.4 %collective-permute-done.26 = f32[384,384]{1,0:T(8,128)S(1)} collective-permute-done((f32[384,384]{1,0:T(8,128)S(1)}, f32[384,384]{1,0:T(8,128)S(1)}, u32[]{:S(2)}, u32[]{:S(2)}) %collective-permute-start.26) | collective-permute-done | bytes 589856 | tf_op jit(solution)/shard_map/U2/ppermute | solution.py:569
  161.5 2.0 collective-permute-start.30
  164.6 1.7 collective-permute-start.32
  167.8 1.8 collective-permute-start.31
  169.7 2.8 %collective-permute-done.30 = f32[224,384]{1,0:T(8,128)S(1)} collective-permute-done((f32[224,384]{1,0:T(8,128)S(1)}, f32[224,384]{1,0:T(8,128)S(1)}, u32[]{:S(2)}, u32[]{:S(2)}) %collective-permute-start.30) | collective-permute-done | bytes 344096 | tf_op jit(solution)/shard_map/S3/ppermute | solution.py:569
  175.3 3.6 %collective-permute-done.31 = f32[192,384]{1,0:T(8,128)S(1)} collective-permute-done((f32[192,384]{1,0:T(8,128)S(1)}, f32[192,384]{1,0:T(8,128)S(1)}, u32[]{:S(2)}, u32[]{:S(2)}) %collective-permute-start.31) | collective-permute-done | bytes 294944 | tf_op jit(solution)/shard_map/R5/ppermute | solution.py:569
  178.9 2.3 collective-permute-start.42
  184.1 10.2 %collective-permute-done.34 = f32[224,384]{1,0:T(8,128)S(1)} collective-permute-done((f32[224,384]{1,0:T(8,128)S(1)}, f32[224,384]{1,0:T(8,128)S(1)}, u32[]{:S(2)}, u32[]{:S(2)}) %collective-permute-start.34) | collective-permute-done | bytes 344096 | tf_op jit(solution)/shard_map/S4/ppermute | solution.py:569
  195.7 2.0 shard_map.324.rest_0_
  197.7 3.5 %collective-permute-start.39 = (f32[192,384]{1,0:T(8,128)S(1)}, f32[192,384]{1,0:T(8,128)S(1)}, u32[]{:S(2)}, u32[]{:S(2)}) collective-permute-start(f32[192,384]{1,0:T(8,128)S(1)} %slice.352), channel_id=1, source_target_pairs={{0,8},{1,9},{2,10},{3,11},{4,12},{5,13},{6,14},{7,15},{8,0},{9,1},... | collective-permute-start | bytes 884744 | tf_op jit(solution)/shard_map/S5/ppermute | solution.py:569
  202.5 2.7 %collective-permute-done.37 = f32[384,384]{1,0:T(8,128)S(1)} collective-permute-done((f32[384,384]{1,0:T(8,128)S(1)}, f32[384,384]{1,0:T(8,128)S(1)}, u32[]{:S(2)}, u32[]{:S(2)}) %collective-permute-start.37) | collective-permute-done | bytes 589856 | tf_op jit(solution)/shard_map/R6/ppermute | solution.py:569
  205.2 6.1 %collective-permute-done.38 = f32[192,384]{1,0:T(8,128)S(1)} collective-permute-done((f32[192,384]{1,0:T(8,128)S(1)}, f32[192,384]{1,0:T(8,128)S(1)}, u32[]{:S(2)}, u32[]{:S(2)}) %collective-permute-start.38) | collective-permute-done | bytes 294944 | tf_op jit(solution)/shard_map/U4/ppermute | solution.py:569
  212.6 1.8 collective-permute-done.39
  215.8 2.3 collective-permute-done.41
  219.6 2.0 shard_map.325.rest_0_
  221.6 8.4 %collective-permute-done.43 = f32[384,384]{1,0:T(8,128)S(1)} collective-permute-done((f32[384,384]{1,0:T(8,128)S(1)}, f32[384,384]{1,0:T(8,128)S(1)}, u32[]{:S(2)}, u32[]{:S(2)}) %collective-permute-start.43) | collective-permute-done | bytes 589856 | tf_op jit(solution)/shard_map/S6/ppermute | solution.py:569
  230.1 1.8 collective-permute-start.46
  234.0 2.0 shard_map.326
  236.0 6.7 %collective-permute-done.45 = f32[384,384]{1,0:T(8,128)S(1)} collective-permute-done((f32[384,384]{1,0:T(8,128)S(1)}, f32[384,384]{1,0:T(8,128)S(1)}, u32[]{:S(2)}, u32[]{:S(2)}) %collective-permute-start.45) | collective-permute-done | bytes 589856 | tf_op jit(solution)/shard_map/U6/ppermute | solution.py:569
  242.7 1.8 collective-permute-start.48
  244.5 2.1 collective-permute-done.46.far
  246.6 2.0 shard_map.327
  248.6 2.0 shard_map.328
  252.5 6.7 %collective-permute-done.48.far = f32[768,384]{1,0:T(8,128)S(1)} collective-permute-done((f32[768,384]{1,0:T(8,128)S(1)}, f32[768,384]{1,0:T(8,128)S(1)}, u32[]{:S(2)}, u32[]{:S(2)}) %collective-permute-start.48) | collective-permute-done | bytes 1179680 | tf_op jit(solution)/shard_map/U7/ppermute | solution.py:569
  259.2 2.0 shard_map.329
  (204 shorter events, 60.6 us)
Async XLA Ops:
  9.5 3.7 %collective-permute-start = (f32[512,768]{1,0:T(8,128)}, f32[512,768]{1,0:T(8,128)S(1)}, u32[]{:S(2)}, u32[]{:S(2)}) collective-permute-start(f32[512,768]{1,0:T(8,128)} %get-tuple-element.119.own), channel_id=1, source_target_pairs={{0,1},{1,0},{2,3},{3,2},{4,5},{5,4},{6,7},{7,6},{8,9},{9,8},{10,11... | collective-permute-start | bytes 4718600 | tf_op jit(solution)/shard_map/ppermute | solution.py:562
  23.0 4.7 %collective-permute-start.1 = (f32[512,768]{1,0:T(8,128)}, f32[512,768]{1,0:T(8,128)S(1)}, u32[]{:S(2)}, u32[]{:S(2)}) collective-permute-start(f32[512,768]{1,0:T(8,128)} %get-tuple-element.121.own), channel_id=1, source_target_pairs={{0,1},{1,0},{2,3},{3,2},{4,5},{5,4},{6,7},{7,6},{8,9},{9,8},{10,11... | collective-permute-start | bytes 4718600 | tf_op jit(solution)/shard_map/ppermute | solution.py:562
  36.5 35.1 %collective-permute-start.6 = (f32[768,384]{1,0:T(8,128)}, f32[768,384]{1,0:T(8,128)S(1)}, u32[]{:S(2)}, u32[]{:S(2)}) collective-permute-start(f32[768,384]{1,0:T(8,128)} %get-tuple-element.127), channel_id=1, source_target_pairs={{0,2},{1,5},{2,0},{3,7},{4,6},{5,1},{6,4},{7,3},{8,10},{9,13},{10,... | collective-permute-start | bytes 3538952 | tf_op jit(solution)/shard_map/E1/ppermute | solution.py:569
  39.1 34.1 %collective-permute-start.7 = (f32[768,384]{1,0:T(8,128)}, f32[768,384]{1,0:T(8,128)S(1)}, u32[]{:S(2)}, u32[]{:S(2)}) collective-permute-start(f32[768,384]{1,0:T(8,128)} %get-tuple-element.126), channel_id=1, source_target_pairs={{0,8},{1,9},{2,10},{3,11},{4,12},{5,13},{6,14},{7,15},{8,0},{9,1},... | collective-permute-start | bytes 3538952 | tf_op jit(solution)/shard_map/D1/ppermute | solution.py:569
  56.2 1.7 collective-permute-start.2
  56.2 2.3 collective-permute-start.3
  56.7 16.5 %collective-permute-start.8 = (f32[768,384]{1,0:T(8,128)S(1)}, f32[768,384]{1,0:T(8,128)S(1)}, u32[]{:S(2)}, u32[]{:S(2)}) collective-permute-start(f32[768,384]{1,0:T(8,128)S(1)} %get-tuple-element.137), channel_id=1, source_target_pairs={{0,2},{1,5},{2,0},{3,7},{4,6},{5,1},{6,4},{7,3},{8,10},{9,13},{10,... | collective-permute-start | bytes 3538952 | tf_op jit(solution)/shard_map/V1/ppermute | solution.py:569
  58.0 1.7 collective-permute-start.4
  71.6 15.4 %collective-permute-start.9 = (f32[384,384]{1,0:T(8,128)S(1)}, f32[384,384]{1,0:T(8,128)S(1)}, u32[]{:S(2)}, u32[]{:S(2)}) collective-permute-start(f32[384,384]{1,0:T(8,128)S(1)} %slice_add_fusion.5), channel_id=1, source_target_pairs={{0,4},{1,3},{2,6},{3,1},{4,0},{5,7},{6,2},{7,5},{8,12},{9,11},{10,... | collective-permute-start | bytes 1769480 | tf_op jit(solution)/shard_map/E2/ppermute | solution.py:569
  73.4 26.3 %collective-permute-start.10 = (f32[384,384]{1,0:T(8,128)S(1)}, f32[384,384]{1,0:T(8,128)S(1)}, u32[]{:S(2)}, u32[]{:S(2)}) collective-permute-start(f32[384,384]{1,0:T(8,128)S(1)} %slice_add_fusion.3), channel_id=1, source_target_pairs={{0,4},{1,3},{2,6},{3,1},{4,0},{5,7},{6,2},{7,5},{8,12},{9,11},{10,... | collective-permute-start | bytes 1769480 | tf_op jit(solution)/shard_map/V2/ppermute | solution.py:569
  74.6 27.8 %collective-permute-start.12 = (f32[384,384]{1,0:T(8,128)S(1)}, f32[384,384]{1,0:T(8,128)S(1)}, u32[]{:S(2)}, u32[]{:S(2)}) collective-permute-start(f32[384,384]{1,0:T(8,128)S(1)} %slice_add_fusion.4), channel_id=1, source_target_pairs={{0,2},{1,5},{2,0},{3,7},{4,6},{5,1},{6,4},{7,3},{8,10},{9,13},{10,... | collective-permute-start | bytes 1769480 | tf_op jit(solution)/shard_map/D2/ppermute | solution.py:569
  75.1 41.0 %collective-permute-start.18 = (f32[800,384]{1,0:T(8,128)S(1)}, f32[800,384]{1,0:T(8,128)S(1)}, u32[]{:S(2)}, u32[]{:S(2)}) collective-permute-start(f32[800,384]{1,0:T(8,128)S(1)} %get-tuple-element.167), channel_id=1, source_target_pairs={{0,2},{1,5},{2,0},{3,7},{4,6},{5,1},{6,4},{7,3},{8,10},{9,13},{10,... | collective-permute-start | bytes 3686408 | tf_op jit(solution)/shard_map/S1/ppermute | solution.py:569
  87.1 14.7 %collective-permute-start.11 = (f32[192,384]{1,0:T(8,128)S(1)}, f32[192,384]{1,0:T(8,128)S(1)}, u32[]{:S(2)}, u32[]{:S(2)}) collective-permute-start(f32[192,384]{1,0:T(8,128)S(1)} %slice_add_fusion.29), channel_id=1, source_target_pairs={{0,8},{1,9},{2,10},{3,11},{4,12},{5,13},{6,14},{7,15},{8,0},{9,1},... | collective-permute-start | bytes 884744 | tf_op jit(solution)/shard_map/E3/ppermute | solution.py:569
  99.7 22.6 %collective-permute-start.15 = (f32[768,384]{1,0:T(8,128)S(1)}, f32[768,384]{1,0:T(8,128)S(1)}, u32[]{:S(2)}, u32[]{:S(2)}) collective-permute-start(f32[768,384]{1,0:T(8,128)S(1)} %get-tuple-element.170), channel_id=1, source_target_pairs={{0,2},{1,5},{2,0},{3,7},{4,6},{5,1},{6,4},{7,3},{8,10},{9,13},{10,... | collective-permute-start | bytes 3538952 | tf_op jit(solution)/shard_map/R1/ppermute | solution.py:569
  100.5 41.5 %collective-permute-start.21 = (f32[768,384]{1,0:T(8,128)}, f32[768,384]{1,0:T(8,128)}, u32[]{:S(2)}, u32[]{:S(2)}) collective-permute-start(f32[768,384]{1,0:T(8,128)} %get-tuple-element.166), channel_id=1, source_target_pairs={{0,2},{1,5},{2,0},{3,7},{4,6},{5,1},{6,4},{7,3},{8,10},{9,13},{10,... | collective-permute-start | bytes 3538952 | tf_op jit(solution)/shard_map/U1/ppermute | solution.py:569
  101.8 9.9 %collective-permute-start.13 = (f32[192,384]{1,0:T(8,128)S(1)}, f32[192,384]{1,0:T(8,128)S(1)}, u32[]{:S(2)}, u32[]{:S(2)}) collective-permute-start(f32[192,384]{1,0:T(8,128)S(1)} %slice_add_fusion.27), channel_id=1, source_target_pairs={{0,8},{1,9},{2,10},{3,11},{4,12},{5,13},{6,14},{7,15},{8,0},{9,1},... | collective-permute-start | bytes 884744 | tf_op jit(solution)/shard_map/V3/ppermute | solution.py:569
  102.4 13.5 %collective-permute-start.14 = (f32[192,384]{1,0:T(8,128)S(1)}, f32[192,384]{1,0:T(8,128)S(1)}, u32[]{:S(2)}, u32[]{:S(2)}) collective-permute-start(f32[192,384]{1,0:T(8,128)S(1)} %fusion.4), channel_id=1, source_target_pairs={{0,24},{1,25},{2,26},{3,27},{4,28},{5,29},{6,30},{7,31},{8,16},{9,... | collective-permute-start | bytes 884744 | tf_op jit(solution)/shard_map/E4/ppermute | solution.py:569
  111.7 17.4 %collective-permute-start.17 = (f32[192,384]{1,0:T(8,128)S(1)}, f32[192,384]{1,0:T(8,128)S(1)}, u32[]{:S(2)}, u32[]{:S(2)}) collective-permute-start(f32[192,384]{1,0:T(8,128)S(1)} %slice_add_fusion.23), channel_id=1, source_target_pairs={{0,4},{1,3},{2,6},{3,1},{4,0},{5,7},{6,2},{7,5},{8,12},{9,11},{10,... | collective-permute-start | bytes 884744 | tf_op jit(solution)/shard_map/D3/ppermute | solution.py:569
  115.9 17.7 %collective-permute-start.19 = (f32[192,384]{1,0:T(8,128)}, f32[192,384]{1,0:T(8,128)}, u32[]{:S(2)}, u32[]{:S(2)}) collective-permute-start(f32[192,384]{1,0:T(8,128)} %fusion.3), channel_id=1, source_target_pairs={{0,24},{1,25},{2,26},{3,27},{4,28},{5,29},{6,30},{7,31},{8,16},{9,... | collective-permute-start | bytes 884744 | tf_op jit(solution)/shard_map/V4/ppermute | solution.py:569
  116.1 12.9 %collective-permute-start.16 = (f32[192,384]{1,0:T(8,128)S(1)}, f32[192,384]{1,0:T(8,128)S(1)}, u32[]{:S(2)}, u32[]{:S(2)}) collective-permute-start(f32[192,384]{1,0:T(8,128)S(1)} %add.164), channel_id=1, source_target_pairs={{0,8},{1,9},{2,10},{3,11},{4,12},{5,13},{6,14},{7,15},{8,0},{9,1},... | collective-permute-start | bytes 884744 | tf_op jit(solution)/shard_map/E5/ppermute | solution.py:569
  123.3 17.6 %collective-permute-start.20 = (f32[384,384]{1,0:T(8,128)}, f32[384,384]{1,0:T(8,128)}, u32[]{:S(2)}, u32[]{:S(2)}) collective-permute-start(f32[384,384]{1,0:T(8,128)} %slice_add_fusion.2), channel_id=1, source_target_pairs={{0,8},{1,9},{2,10},{3,11},{4,12},{5,13},{6,14},{7,15},{8,0},{9,1},... | collective-permute-start | bytes 1769480 | tf_op jit(solution)/shard_map/R2/ppermute | solution.py:569
  130.8 14.3 %collective-permute-start.25 = (f32[416,384]{1,0:T(8,128)}, f32[416,384]{1,0:T(8,128)}, u32[]{:S(2)}, u32[]{:S(2)}) collective-permute-start(f32[416,384]{1,0:T(8,128)} %pad_maximum_fusion), channel_id=1, source_target_pairs={{0,4},{1,3},{2,6},{3,1},{4,0},{5,7},{6,2},{7,5},{8,12},{9,11},{10,... | collective-permute-start | bytes 1916936 | tf_op jit(solution)/shard_map/S2/ppermute | solution.py:569
  133.5 64.1 %collective-permute-start.36 = (f32[512,768]{1,0:T(8,128)S(1)}, f32[512,768]{1,0:T(8,128)S(1)}, u32[]{:S(2)}, u32[]{:S(2)}) collective-permute-start(f32[512,768]{1,0:T(8,128)S(1)} %shard_map.323), channel_id=1, source_target_pairs={{0,1},{1,0},{2,3},{3,2},{4,5},{5,4},{6,7},{7,6},{8,9},{9,8},{10,11... | collective-permute-start | bytes 4718600 | tf_op jit(solution)/shard_map/ppermute | solution.py:562
  133.6 18.3 %collective-permute-start.23 = (f32[192,384]{1,0:T(8,128)S(1)}, f32[192,384]{1,0:T(8,128)S(1)}, u32[]{:S(2)}, u32[]{:S(2)}) collective-permute-start(f32[192,384]{1,0:T(8,128)S(1)} %fusion.2), channel_id=1, source_target_pairs={{0,24},{1,25},{2,26},{3,27},{4,28},{5,29},{6,30},{7,31},{8,16},{9,... | collective-permute-start | bytes 884744 | tf_op jit(solution)/shard_map/D4/ppermute | solution.py:569
  140.9 13.8 %collective-permute-start.24 = (f32[192,384]{1,0:T(8,128)S(1)}, f32[192,384]{1,0:T(8,128)S(1)}, u32[]{:S(2)}, u32[]{:S(2)}) collective-permute-start(f32[192,384]{1,0:T(8,128)S(1)} %add.171), channel_id=1, source_target_pairs={{0,8},{1,9},{2,10},{3,11},{4,12},{5,13},{6,14},{7,15},{8,0},{9,1},... | collective-permute-start | bytes 884744 | tf_op jit(solution)/shard_map/V5/ppermute | solution.py:569
  142.1 6.8 %collective-permute-start.22 = (f32[192,384]{1,0:T(8,128)S(1)}, f32[192,384]{1,0:T(8,128)S(1)}, u32[]{:S(2)}, u32[]{:S(2)}) collective-permute-start(f32[192,384]{1,0:T(8,128)S(1)} %slice_add_fusion.17), channel_id=1, source_target_pairs={{0,4},{1,3},{2,6},{3,1},{4,0},{5,7},{6,2},{7,5},{8,12},{9,11},{10,... | collective-permute-start | bytes 884744 | tf_op jit(solution)/shard_map/R3/ppermute | solution.py:569
  145.1 19.5 %collective-permute-start.27 = (f32[384,384]{1,0:T(8,128)S(1)}, f32[384,384]{1,0:T(8,128)S(1)}, u32[]{:S(2)}, u32[]{:S(2)}) collective-permute-start(f32[384,384]{1,0:T(8,128)S(1)} %copy-done.34), channel_id=1, source_target_pairs={{0,4},{1,3},{2,6},{3,1},{4,0},{5,7},{6,2},{7,5},{8,12},{9,11},{10,... | collective-permute-start | bytes 1769480 | tf_op jit(solution)/shard_map/E6/ppermute | solution.py:569
  148.9 12.6 %collective-permute-start.26 = (f32[384,384]{1,0:T(8,128)S(1)}, f32[384,384]{1,0:T(8,128)S(1)}, u32[]{:S(2)}, u32[]{:S(2)}) collective-permute-start(f32[384,384]{1,0:T(8,128)S(1)} %slice_add_fusion), channel_id=1, source_target_pairs={{0,4},{1,3},{2,6},{3,1},{4,0},{5,7},{6,2},{7,5},{8,12},{9,11},{10,... | collective-permute-start | bytes 1769480 | tf_op jit(solution)/shard_map/U2/ppermute | solution.py:569
  151.9 14.5 %collective-permute-start.28 = (f32[192,384]{1,0:T(8,128)S(1)}, f32[192,384]{1,0:T(8,128)S(1)}, u32[]{:S(2)}, u32[]{:S(2)}) collective-permute-start(f32[192,384]{1,0:T(8,128)S(1)} %fusion.1), channel_id=1, source_target_pairs={{0,24},{1,25},{2,26},{3,27},{4,28},{5,29},{6,30},{7,31},{8,16},{9,... | collective-permute-start | bytes 884744 | tf_op jit(solution)/shard_map/R4/ppermute | solution.py:569
  154.7 13.1 %collective-permute-start.29 = (f32[384,384]{1,0:T(8,128)S(1)}, f32[384,384]{1,0:T(8,128)S(1)}, u32[]{:S(2)}, u32[]{:S(2)}) collective-permute-start(f32[384,384]{1,0:T(8,128)S(1)} %constant_dynamic-update-slice_fusion.2), channel_id=1, source_target_pairs={{0,4},{1,3},{2,6},{3,1},{4,0},{5,7},{6,2},{7,5},{8,12},{9,11},{10,... | collective-permute-start | bytes 1769480 | tf_op jit(solution)/shard_map/V6/ppermute | solution.py:569
  161.5 11.0 %collective-permute-start.30 = (f32[224,384]{1,0:T(8,128)S(1)}, f32[224,384]{1,0:T(8,128)S(1)}, u32[]{:S(2)}, u32[]{:S(2)}) collective-permute-start(f32[224,384]{1,0:T(8,128)S(1)} %pad_maximum_fusion.1), channel_id=1, source_target_pairs={{0,8},{1,9},{2,10},{3,11},{4,12},{5,13},{6,14},{7,15},{8,0},{9,1},... | collective-permute-start | bytes 1032200 | tf_op jit(solution)/shard_map/S3/ppermute | solution.py:569
  164.6 16.7 %collective-permute-start.32 = (f32[192,384]{1,0:T(8,128)S(1)}, f32[192,384]{1,0:T(8,128)S(1)}, u32[]{:S(2)}, u32[]{:S(2)}) collective-permute-start(f32[192,384]{1,0:T(8,128)S(1)} %add.178), channel_id=1, source_target_pairs={{0,4},{1,3},{2,6},{3,1},{4,0},{5,7},{6,2},{7,5},{8,12},{9,11},{10,... | collective-permute-start | bytes 884744 | tf_op jit(solution)/shard_map/D5/ppermute | solution.py:569
  166.4 15.6 %collective-permute-start.33 = (f32[192,384]{1,0:T(8,128)S(1)}, f32[192,384]{1,0:T(8,128)S(1)}, u32[]{:S(2)}, u32[]{:S(2)}) collective-permute-start(f32[192,384]{1,0:T(8,128)S(1)} %slice_add_fusion.11), channel_id=1, source_target_pairs={{0,8},{1,9},{2,10},{3,11},{4,12},{5,13},{6,14},{7,15},{8,0},{9,1},... | collective-permute-start | bytes 884744 | tf_op jit(solution)/shard_map/U3/ppermute | solution.py:569
  167.8 11.1 %collective-permute-start.31 = (f32[192,384]{1,0:T(8,128)S(1)}, f32[192,384]{1,0:T(8,128)S(1)}, u32[]{:S(2)}, u32[]{:S(2)}) collective-permute-start(f32[192,384]{1,0:T(8,128)S(1)} %add.184), channel_id=1, source_target_pairs={{0,4},{1,3},{2,6},{3,1},{4,0},{5,7},{6,2},{7,5},{8,12},{9,11},{10,... | collective-permute-start | bytes 884744 | tf_op jit(solution)/shard_map/R5/ppermute | solution.py:569
  172.5 22.3 %collective-permute-start.35 = (f32[768,384]{1,0:T(8,128)S(1)}, f32[768,384]{1,0:T(8,128)S(1)}, u32[]{:S(2)}, u32[]{:S(2)}) collective-permute-start(f32[768,384]{1,0:T(8,128)S(1)} %constant_dynamic-update-slice_fusion.6.near), channel_id=1, source_target_pairs={{0,2},{1,5},{2,0},{3,7},{4,6},{5,1},{6,4},{7,3},{8,10},{9,13},{10,... | collective-permute-start | bytes 3538952 | tf_op jit(solution)/shard_map/V7/ppermute | solution.py:569
  178.9 40.7 %collective-permute-start.42 = (f32[768,384]{1,0:T(8,128)S(1)}, f32[768,384]{1,0:T(8,128)S(1)}, u32[]{:S(2)}, u32[]{:S(2)}) collective-permute-start(f32[768,384]{1,0:T(8,128)S(1)} %constant_dynamic-update-slice_fusion.4.near), channel_id=1, source_target_pairs={{0,2},{1,5},{2,0},{3,7},{4,6},{5,1},{6,4},{7,3},{8,10},{9,13},{10,... | collective-permute-start | bytes 3538952 | tf_op jit(solution)/shard_map/E7/ppermute | solution.py:569
  181.3 13.0 %collective-permute-start.34 = (f32[224,384]{1,0:T(8,128)S(1)}, f32[224,384]{1,0:T(8,128)S(1)}, u32[]{:S(2)}, u32[]{:S(2)}) collective-permute-start(f32[224,384]{1,0:T(8,128)S(1)} %pad_maximum_fusion.2), channel_id=1, source_target_pairs={{0,24},{1,25},{2,26},{3,27},{4,28},{5,29},{6,30},{7,31},{8,16},{9,... | collective-permute-start | bytes 1032200 | tf_op jit(solution)/shard_map/S4/ppermute | solution.py:569
  182.0 23.2 %collective-permute-start.37 = (f32[384,384]{1,0:T(8,128)S(1)}, f32[384,384]{1,0:T(8,128)S(1)}, u32[]{:S(2)}, u32[]{:S(2)}) collective-permute-start(f32[384,384]{1,0:T(8,128)S(1)} %constant_dynamic-update-slice_fusion.8), channel_id=1, source_target_pairs={{0,8},{1,9},{2,10},{3,11},{4,12},{5,13},{6,14},{7,15},{8,0},{9,1},... | collective-permute-start | bytes 1769480 | tf_op jit(solution)/shard_map/R6/ppermute | solution.py:569
  194.3 17.0 %collective-permute-start.38 = (f32[192,384]{1,0:T(8,128)S(1)}, f32[192,384]{1,0:T(8,128)S(1)}, u32[]{:S(2)}, u32[]{:S(2)}) collective-permute-start(f32[192,384]{1,0:T(8,128)S(1)} %fusion), channel_id=1, source_target_pairs={{0,24},{1,25},{2,26},{3,27},{4,28},{5,29},{6,30},{7,31},{8,16},{9,... | collective-permute-start | bytes 884744 | tf_op jit(solution)/shard_map/U4/ppermute | solution.py:569
  194.8 20.9 %collective-permute-start.40 = (f32[384,384]{1,0:T(8,128)S(1)}, f32[384,384]{1,0:T(8,128)S(1)}, u32[]{:S(2)}, u32[]{:S(2)}) collective-permute-start(f32[384,384]{1,0:T(8,128)S(1)} %constant_dynamic-update-slice_fusion.10), channel_id=1, source_target_pairs={{0,2},{1,5},{2,0},{3,7},{4,6},{5,1},{6,4},{7,3},{8,10},{9,13},{10,... | collective-permute-start | bytes 1769480 | tf_op jit(solution)/shard_map/D6/ppermute | solution.py:569
  197.7 16.6 %collective-permute-start.39 = (f32[192,384]{1,0:T(8,128)S(1)}, f32[192,384]{1,0:T(8,128)S(1)}, u32[]{:S(2)}, u32[]{:S(2)}) collective-permute-start(f32[192,384]{1,0:T(8,128)S(1)} %slice.352), channel_id=1, source_target_pairs={{0,8},{1,9},{2,10},{3,11},{4,12},{5,13},{6,14},{7,15},{8,0},{9,1},... | collective-permute-start | bytes 884744 | tf_op jit(solution)/shard_map/S5/ppermute | solution.py:569
  211.3 6.8 %collective-permute-start.41 = (f32[192,384]{1,0:T(8,128)S(1)}, f32[192,384]{1,0:T(8,128)S(1)}, u32[]{:S(2)}, u32[]{:S(2)}) collective-permute-start(f32[192,384]{1,0:T(8,128)S(1)} %add.195), channel_id=1, source_target_pairs={{0,8},{1,9},{2,10},{3,11},{4,12},{5,13},{6,14},{7,15},{8,0},{9,1},... | collective-permute-start | bytes 884744 | tf_op jit(solution)/shard_map/U5/ppermute | solution.py:569
  211.4 22.6 %collective-permute-start.44 = (f32[768,384]{1,0:T(8,128)S(1)}, f32[768,384]{1,0:T(8,128)S(1)}, u32[]{:S(2)}, u32[]{:S(2)}) collective-permute-start(f32[768,384]{1,0:T(8,128)S(1)} %constant_dynamic-update-slice_fusion.12.near), channel_id=1, source_target_pairs={{0,2},{1,5},{2,0},{3,7},{4,6},{5,1},{6,4},{7,3},{8,10},{9,13},{10,... | collective-permute-start | bytes 3538952 | tf_op jit(solution)/shard_map/R7/ppermute | solution.py:569
  214.3 15.7 %collective-permute-start.43 = (f32[384,384]{1,0:T(8,128)S(1)}, f32[384,384]{1,0:T(8,128)S(1)}, u32[]{:S(2)}, u32[]{:S(2)}) collective-permute-start(f32[384,384]{1,0:T(8,128)S(1)} %constant_dynamic-update-slice_fusion.14), channel_id=1, source_target_pairs={{0,4},{1,3},{2,6},{3,1},{4,0},{5,7},{6,2},{7,5},{8,12},{9,11},{10,... | collective-permute-start | bytes 1769480 | tf_op jit(solution)/shard_map/S6/ppermute | solution.py:569
  218.1 24.6 %collective-permute-start.45 = (f32[384,384]{1,0:T(8,128)S(1)}, f32[384,384]{1,0:T(8,128)S(1)}, u32[]{:S(2)}, u32[]{:S(2)}) collective-permute-start(f32[384,384]{1,0:T(8,128)S(1)} %constant_dynamic-update-slice_fusion.18), channel_id=1, source_target_pairs={{0,4},{1,3},{2,6},{3,1},{4,0},{5,7},{6,2},{7,5},{8,12},{9,11},{10,... | collective-permute-start | bytes 1769480 | tf_op jit(solution)/shard_map/U6/ppermute | solution.py:569
  230.1 16.5 %collective-permute-start.46 = (f32[768,384]{1,0:T(8,128)S(1)}, f32[768,384]{1,0:T(8,128)S(1)}, u32[]{:S(2)}, u32[]{:S(2)}) collective-permute-start(f32[768,384]{1,0:T(8,128)S(1)} %constant_dynamic-update-slice_fusion.20.near), channel_id=1, source_target_pairs={{0,2},{1,5},{2,0},{3,7},{4,6},{5,1},{6,4},{7,3},{8,10},{9,13},{10,... | collective-permute-start | bytes 3538952 | tf_op jit(solution)/shard_map/S7/ppermute | solution.py:569
  231.9 16.7 %collective-permute-start.47 = (f32[768,384]{1,0:T(8,128)S(1)}, f32[768,384]{1,0:T(8,128)S(1)}, u32[]{:S(2)}, u32[]{:S(2)}) collective-permute-start(f32[768,384]{1,0:T(8,128)S(1)} %constant_dynamic-update-slice_fusion.16.near), channel_id=1, source_target_pairs={{0,8},{1,9},{2,10},{3,11},{4,12},{5,13},{6,14},{7,15},{8,0},{9,1},... | collective-permute-start | bytes 3538952 | tf_op jit(solution)/shard_map/D7/ppermute | solution.py:569
  242.7 16.5 %collective-permute-start.48 = (f32[768,384]{1,0:T(8,128)S(1)}, f32[768,384]{1,0:T(8,128)S(1)}, u32[]{:S(2)}, u32[]{:S(2)}) collective-permute-start(f32[768,384]{1,0:T(8,128)S(1)} %constant_dynamic-update-slice_fusion.22.near), channel_id=1, source_target_pairs={{0,2},{1,5},{2,0},{3,7},{4,6},{5,1},{6,4},{7,3},{8,10},{9,13},{10,... | collective-permute-start | bytes 3538952 | tf_op jit(solution)/shard_map/U7/ppermute | solution.py:569
  (38 other events, 341.8 us)
